TPU v7x, 32 devices: a whole 2x2x4 slice. The times are simulated.
32 devices in a mesh: dom: 32 (over z, y, x, core).
Axes of the slice: x: 2, y: 2, z: 4, core: 2. Of those that a mesh axis runs over, the one named last changes fastest.
Arguments:
- grad_out: bfloat16 [16384, 256], P('dom'), may hold values from -6 to 6
- states: bfloat16 [16384, 256], P('dom'), may hold values from -0.98828125 to 0.98828125
- slopes: bfloat16 [16384, 256], P('dom'), may hold values from 0.099609375 to 1
- weight: bfloat16 [256, 256], replicated, may hold values from -0.375 to 0.375
- tiles: bfloat16 [768, 128, 128], P('dom'), may hold values from -0.23925781 to 0.23925781
- tile_dst: int32 [768], P('dom'), may hold values from 0 to 3, as said below
- tile_src: int32 [768], P('dom'), may hold values from 0 to 7, as said below
- tile_count: int32 [32], P('dom'), may hold values from 12 to 24, as said below
- send_rows: int32 [128, 128], P('dom'), may hold values from 0 to 511, as said below
Outputs:
- adjoint: float32 [16384, 256], P('dom')
- weight_grad: float32 [256, 256], replicated
Inputs may be any that keep to these rules, and one draw needn't show every extreme that they name: `tile_src`: slot s of a partition with s < 4 has source tile 4 + s; slots 4 to 7 have destination and source tile s - 4; other used slots name a destination below 4 and a source below 8. `tile_dst`: destination tiles of a partition's slots. `tile_count`: some partition uses all 24 slots. `send_rows`: each list holds distinct local rows.
All inputs are finite; a program needn't handle non-finite values.
Results may differ from a plain program's by a relative error of at most 0.009.
Values may be sent and summed in bfloat16 or wider, within the bound.
No kernel may reach another device: no remote copies, remote signals or barrier semaphores. Data moves between devices by JAX's collectives and lax.ppermute only.
A program may use at most 64 MiB of HBM per device.

v0:
```python
import jax
import jax.numpy as jnp
from jax import lax
from jax.sharding import PartitionSpec as P

ITERS = 4


neighbour_steps = (1, -1, 16, -16)


def passed_along(value, axis, steps):
    count = lax.axis_size(axis)
    pairs = [(source, (source + steps) % count) for source in range(count)]
    return lax.ppermute(value, axis, pairs)


def add_tiles(tiles, tile_dst, tile_src, count, extended, total, keep):
    size = tiles.shape[1]
    width = extended.shape[1]
    sources = extended.shape[0] // size
    blocks = total.shape[0] // size
    slots = tiles.shape[0]
    stacked = extended.reshape(sources, size, width)
    index = jnp.minimum(tile_src, sources - 1)
    rows = jnp.take(stacked, index, axis=0)
    prod = jnp.einsum("tij,tjh->tih", tiles, rows, preferred_element_type=jnp.float32)
    used = (jnp.arange(slots, dtype=jnp.int32) < count) & keep(tile_src)
    onehot = (
        (tile_dst[None, :] == jnp.arange(blocks, dtype=jnp.int32)[:, None]) & used[None, :]
    ).astype(jnp.float32)
    summed = jnp.dot(onehot, prod.reshape(slots, size * width), precision=lax.Precision.HIGHEST)
    return summed.reshape(blocks * size, width)


def with_boundary(scaled, send_rows):
    pieces = [scaled]
    for direction in range(4):
        chosen = jnp.take(scaled, send_rows[direction], axis=0)
        pieces.append(passed_along(chosen, "dom", neighbour_steps[direction]))
    return jnp.concatenate(pieces, axis=0)


def propagate(scaled, tiles, tile_dst, tile_src, count, send_rows):
    empty = jnp.zeros(scaled.shape, jnp.float32)
    extended = with_boundary(scaled, send_rows)
    return add_tiles(tiles, tile_dst, tile_src, count, extended, empty, lambda s: s >= 0)


def per_device(grad_out, states, slopes, weight, tiles, tile_dst, tile_src, tile_count, send_rows):
    count = tile_count[0]
    slope_values = slopes.astype(jnp.float32)
    base = grad_out.astype(jnp.float32)
    adjoint = base
    for step in range(ITERS):
        scaled = (slope_values * adjoint).astype(jnp.bfloat16)
        mixed = propagate(scaled, tiles, tile_dst, tile_src, count, send_rows).astype(jnp.bfloat16)
        adjoint = base + lax.dot_general(
            mixed, weight, (((1,), (1,)), ((), ())), preferred_element_type=jnp.float32
        )
    final_scaled = (slope_values * adjoint).astype(jnp.bfloat16)
    node_total = lax.axis_size("dom") * grad_out.shape[0]
    factor = 1.0 / jnp.sqrt(jnp.float32(node_total))
    state_values = states.astype(jnp.float32)
    final_mixed = propagate(final_scaled, tiles, tile_dst, tile_src, count, send_rows)
    grad = lax.psum(
        lax.dot_general(
            state_values, final_mixed, (((0,), (0,)), ((), ())), precision=lax.Precision.HIGHEST
        )
        * factor,
        "dom",
    )
    return (adjoint, grad)


def solution(mesh):
    in_specs = (
        P("dom", None),
        P("dom", None),
        P("dom", None),
        P(),
        P("dom", None, None),
        P("dom"),
        P("dom"),
        P("dom"),
        P("dom", None),
    )
    out_specs = (P("dom", None), P())
    return jax.shard_map(
        per_device, mesh=mesh, in_specs=in_specs, out_specs=out_specs, check_vma=False
    )
```

profile of v0, /device:TPU:0, one launch (start us, length us, event | category | flops | bytes accessed | tf_op | source)
XLA Modules:
  0.0 283.6 jit_solution(12685391604185503891)
XLA Ops:
  8.1 1.1 constant_dynamic-update-slice_fusion.4
  10.1 6.5 %collective-permute-start.1 = (bf16[128,256]{1,0:T(8,128)(2,1)S(1)}, bf16[128,256]{1,0:T(8,128)(2,1)S(1)}, u32[]{:S(2)}, u32[]{:S(2)}) collective-permute-start(bf16[128,256]{1,0:T(8,128)(2,1)S(1)} %broadcast_select_fusion.14), channel_id=1, source_target_pairs={{0,31},{1,0},{2,1},{3,2},{4,3},{5,4},{6,5},{7,6},{8,7},{9,8},{10,9... | collective-permute-start | bytes 196616 | tf_op jit(solution)/shard_map/ppermute | solution.py:15
  17.6 0.8 gather_fusion.2
  19.6 3.0 %collective-permute-start.3 = (bf16[128,256]{1,0:T(8,128)(2,1)S(1)}, bf16[128,256]{1,0:T(8,128)(2,1)S(1)}, u32[]{:S(2)}, u32[]{:S(2)}) collective-permute-start(bf16[128,256]{1,0:T(8,128)(2,1)S(1)} %broadcast_select_fusion.4), channel_id=1, source_target_pairs={{0,16},{1,17},{2,18},{3,19},{4,20},{5,21},{6,22},{7,23},{8,24},{9,... | collective-permute-start | bytes 196616 | tf_op jit(solution)/shard_map/ppermute | solution.py:15
  23.3 1.7 collective-permute-done
  25.0 0.9 collective-permute-done.3
  26.6 2.3 convolution_bitcast_fusion.4
  28.9 3.6 %copy.28 = f32[3,8,128,256]{3,1,2,0:T(8,128)} copy(f32[3,8,128,256]{2,3,1,0:T(8,128)} %bitcast.77) | data formatting | bytes 6291456
  32.5 3.1 %convolution_convert_fusion.3 = bf16[4,32768]{1,0:T(4,128)(2,1)S(1)} fusion(pred[4,24]{1,0:T(4,128)(4,1)S(1)} %fusion.24, f32[24,32768]{1,0:T(8,128)} %bitcast.71), kind=kOutput, calls=%fused_computation.28 | convolution fusion | flops 37879808 | bytes 3407968 | tf_op jit(solution)/shard_map/dot_general | solution.py:32
  37.8 0.8 gather_fusion.6
  38.7 0.8 gather_fusion.5
  39.9 5.4 %collective-permute-start.5 = (bf16[128,256]{1,0:T(8,128)(2,1)S(1)}, bf16[128,256]{1,0:T(8,128)(2,1)S(1)}, u32[]{:S(2)}, u32[]{:S(2)}) collective-permute-start(bf16[128,256]{1,0:T(8,128)(2,1)S(1)} %broadcast_select_fusion.13), channel_id=1, source_target_pairs={{0,31},{1,0},{2,1},{3,2},{4,3},{5,4},{6,5},{7,6},{8,7},{9,8},{10,9... | collective-permute-start | bytes 196616 | tf_op jit(solution)/shard_map/ppermute | solution.py:15
  45.4 2.9 %collective-permute-start.7 = (bf16[128,256]{1,0:T(8,128)(2,1)S(1)}, bf16[128,256]{1,0:T(8,128)(2,1)S(1)}, u32[]{:S(2)}, u32[]{:S(2)}) collective-permute-start(bf16[128,256]{1,0:T(8,128)(2,1)S(1)} %broadcast_select_fusion.3), channel_id=1, source_target_pairs={{0,16},{1,17},{2,18},{3,19},{4,20},{5,21},{6,22},{7,23},{8,24},{9,... | collective-permute-start | bytes 196616 | tf_op jit(solution)/shard_map/ppermute | solution.py:15
  48.3 2.8 collective-permute-done.6
  51.8 1.9 gather_fusion.9
  53.6 3.7 %convolution_bitcast_fusion.3 = f32[24,128,256]{1,2,0:T(8,128)} fusion(bf16[24,128,128]{2,1,0:T(8,128)(2,1)S(1)} %copy-done, bf16[24,128,256]{2,1,0:T(8,128)(2,1)} %gather_fusion.9, pred[24]{0:T(512)(128)(4,1)S(1)} %get-tuple-element.10), kind=kOutput, calls=%fused_computation.32 | convolution fusion | flops 202113024 | bytes 5505048 | tf_op jit(solution)/shard_map/tij,tjh->tih/dot_general | solution.py:27
  57.4 3.6 %copy.29 = f32[3,8,128,256]{3,1,2,0:T(8,128)} copy(f32[3,8,128,256]{2,3,1,0:T(8,128)} %bitcast.78) | data formatting | bytes 6291456
  60.9 3.1 %convolution_convert_fusion.2 = bf16[4,32768]{1,0:T(4,128)(2,1)S(1)} fusion(pred[4,24]{1,0:T(4,128)(4,1)S(1)} %fusion.24, f32[24,32768]{1,0:T(8,128)} %bitcast.72), kind=kOutput, calls=%fused_computation.27 | convolution fusion | flops 37879808 | bytes 3407968 | tf_op jit(solution)/shard_map/dot_general | solution.py:32
  64.5 0.8 gather_fusion.13
  67.0 0.8 gather_fusion.10
  68.3 5.6 %collective-permute-start.9 = (bf16[128,256]{1,0:T(8,128)(2,1)S(1)}, bf16[128,256]{1,0:T(8,128)(2,1)S(1)}, u32[]{:S(2)}, u32[]{:S(2)}) collective-permute-start(bf16[128,256]{1,0:T(8,128)(2,1)S(1)} %broadcast_select_fusion.12), channel_id=1, source_target_pairs={{0,31},{1,0},{2,1},{3,2},{4,3},{5,4},{6,5},{7,6},{8,7},{9,8},{10,9... | collective-permute-start | bytes 196616 | tf_op jit(solution)/shard_map/ppermute | solution.py:15
  73.9 2.9 %collective-permute-start.11 = (bf16[128,256]{1,0:T(8,128)(2,1)S(1)}, bf16[128,256]{1,0:T(8,128)(2,1)S(1)}, u32[]{:S(2)}, u32[]{:S(2)}) collective-permute-start(bf16[128,256]{1,0:T(8,128)(2,1)S(1)} %broadcast_select_fusion.2), channel_id=1, source_target_pairs={{0,16},{1,17},{2,18},{3,19},{4,20},{5,21},{6,22},{7,23},{8,24},{9,... | collective-permute-start | bytes 196616 | tf_op jit(solution)/shard_map/ppermute | solution.py:15
  76.8 2.2 collective-permute-done.10
  79.7 1.9 gather_fusion.14
  81.6 3.7 %convolution_bitcast_fusion.2 = f32[24,128,256]{1,2,0:T(8,128)} fusion(bf16[24,128,128]{2,1,0:T(8,128)(2,1)S(1)} %copy-done, bf16[24,128,256]{2,1,0:T(8,128)(2,1)} %gather_fusion.14, pred[24]{0:T(512)(128)(4,1)S(1)} %get-tuple-element.10), kind=kOutput, calls=%fused_computation.31 | convolution fusion | flops 202113024 | bytes 5505048 | tf_op jit(solution)/shard_map/tij,tjh->tih/dot_general | solution.py:27
  85.3 3.6 %copy.30 = f32[3,8,128,256]{3,1,2,0:T(8,128)} copy(f32[3,8,128,256]{2,3,1,0:T(8,128)} %bitcast.79) | data formatting | bytes 6291456
  88.9 3.1 %convolution_convert_fusion.1 = bf16[4,32768]{1,0:T(4,128)(2,1)S(1)} fusion(pred[4,24]{1,0:T(4,128)(4,1)S(1)} %fusion.24, f32[24,32768]{1,0:T(8,128)} %bitcast.73), kind=kOutput, calls=%fused_computation.26 | convolution fusion | flops 37879808 | bytes 3407968 | tf_op jit(solution)/shard_map/dot_general | solution.py:32
  92.4 0.8 gather_fusion.18
  95.0 0.8 gather_fusion.15
  96.2 5.4 %collective-permute-start.13 = (bf16[128,256]{1,0:T(8,128)(2,1)S(1)}, bf16[128,256]{1,0:T(8,128)(2,1)S(1)}, u32[]{:S(2)}, u32[]{:S(2)}) collective-permute-start(bf16[128,256]{1,0:T(8,128)(2,1)S(1)} %broadcast_select_fusion.11), channel_id=1, source_target_pairs={{0,31},{1,0},{2,1},{3,2},{4,3},{5,4},{6,5},{7,6},{8,7},{9,8},{10,9... | collective-permute-start | bytes 196616 | tf_op jit(solution)/shard_map/ppermute | solution.py:15
  102.1 2.5 collective-permute-start.15
  104.6 2.2 collective-permute-done.14
  107.5 1.9 gather_fusion.19
  109.4 3.7 %convolution_bitcast_fusion.1 = f32[24,128,256]{1,2,0:T(8,128)} fusion(bf16[24,128,128]{2,1,0:T(8,128)(2,1)S(1)} %copy-done, bf16[24,128,256]{2,1,0:T(8,128)(2,1)} %gather_fusion.19, pred[24]{0:T(512)(128)(4,1)S(1)} %get-tuple-element.10), kind=kOutput, calls=%fused_computation.30 | convolution fusion | flops 202113024 | bytes 5505048 | tf_op jit(solution)/shard_map/tij,tjh->tih/dot_general | solution.py:27
  113.1 3.6 %copy.31 = f32[3,8,128,256]{3,1,2,0:T(8,128)} copy(f32[3,8,128,256]{2,3,1,0:T(8,128)} %bitcast.80) | data formatting | bytes 6291456
  116.7 3.1 %convolution_convert_fusion = bf16[4,32768]{1,0:T(4,128)(2,1)S(1)} fusion(pred[4,24]{1,0:T(4,128)(4,1)S(1)} %fusion.24, f32[24,32768]{1,0:T(8,128)} %bitcast.74), kind=kOutput, calls=%fused_computation.25 | convolution fusion | flops 37879808 | bytes 3407968 | tf_op jit(solution)/shard_map/dot_general | solution.py:32
  119.9 1.1 constant_dynamic-update-slice_fusion.24
  122.7 0.8 gather_fusion.21
  124.8 5.6 %collective-permute-start.17 = (bf16[128,256]{1,0:T(8,128)(2,1)S(1)}, bf16[128,256]{1,0:T(8,128)(2,1)S(1)}, u32[]{:S(2)}, u32[]{:S(2)}) collective-permute-start(bf16[128,256]{1,0:T(8,128)(2,1)S(1)} %broadcast_select_fusion.10), channel_id=1, source_target_pairs={{0,31},{1,0},{2,1},{3,2},{4,3},{5,4},{6,5},{7,6},{8,7},{9,8},{10,9... | collective-permute-start | bytes 196616 | tf_op jit(solution)/shard_map/ppermute | solution.py:15
  130.8 2.5 collective-permute-start.19
  133.4 2.2 collective-permute-done.18
  136.3 1.9 gather_fusion.24
  138.1 3.7 %convolution_bitcast_fusion = f32[24,128,256]{1,2,0:T(8,128)} fusion(bf16[24,128,128]{2,1,0:T(8,128)(2,1)S(1)} %copy-done, bf16[24,128,256]{2,1,0:T(8,128)(2,1)} %gather_fusion.24, pred[24]{0:T(512)(128)(4,1)S(1)} %get-tuple-element.10), kind=kOutput, calls=%fused_computation.29 | convolution fusion | flops 202113024 | bytes 5505048 | tf_op jit(solution)/shard_map/tij,tjh->tih/dot_general | solution.py:27
  141.9 3.6 %copy.32 = f32[3,8,128,256]{3,1,2,0:T(8,128)} copy(f32[3,8,128,256]{2,3,1,0:T(8,128)} %bitcast.75) | data formatting | bytes 6291456
  145.4 3.1 %fusion.32 = f32[4,32768]{1,0:T(4,128)S(1)} fusion(pred[4,24]{1,0:T(4,128)(4,1)S(1)} %fusion.24, f32[24,32768]{1,0:T(8,128)} %bitcast.76), kind=kOutput, calls=%fused_computation.133 | convolution fusion | flops 37748736 | bytes 3670112 | tf_op jit(solution)/shard_map/dot_general | solution.py:32
  148.9 1.3 fusion.16
  150.2 124.7 %all-reduce.2.cloned.1.call-done = f32[256,256]{0,1:T(8,128)} async-done(((f32[256,256]{0,1:T(8,128)}), f32[256,256]{0,1:T(8,128)}) %all-reduce.2.cloned.1.call-update) | async-done | bytes 262160 | tf_op jit(solution)/shard_map/psum | solution.py:66
  275.0 1.8 copy.22
  (109 shorter events, 19.5 us)
Async XLA Ops:
  7.2 19.4 %copy-start = (bf16[24,128,128]{2,1,0:T(8,128)(2,1)S(1)}, bf16[24,128,128]{2,1,0:T(8,128)(2,1)}, u32[]{:S(2)}) copy-start(bf16[24,128,128]{2,1,0:T(8,128)(2,1)} %param.17) | copy-start | bytes 2359300
  7.2 267.8 %all-reduce.2.cloned.1.call-start = ((), (), s32[]{:S(2)}) async-start(), calls=%async_computation | async-start | bytes 524288 | tf_op jit(solution)/shard_map/psum | solution.py:66
  9.2 14.0 %copy-start.5 = (s32[24]{0:T(128)S(1)}, s32[24]{0:T(128)}, u32[]{:S(2)}) copy-start(s32[24]{0:T(128)} %param.19) | copy-start | bytes 292
  9.2 14.1 %copy-start.6 = (s32[24]{0:T(128)S(1)}, s32[24]{0:T(128)}, u32[]{:S(2)}) copy-start(s32[24]{0:T(128)} %param.18) | copy-start | bytes 292
  10.1 14.8 %collective-permute-start.1 = (bf16[128,256]{1,0:T(8,128)(2,1)S(1)}, bf16[128,256]{1,0:T(8,128)(2,1)S(1)}, u32[]{:S(2)}, u32[]{:S(2)}) collective-permute-start(bf16[128,256]{1,0:T(8,128)(2,1)S(1)} %broadcast_select_fusion.14), channel_id=1, source_target_pairs={{0,31},{1,0},{2,1},{3,2},{4,3},{5,4},{6,5},{7,6},{8,7},{9,8},{10,9... | collective-permute-start | bytes 196616 | tf_op jit(solution)/shard_map/ppermute | solution.py:15
  17.5 7.4 %collective-permute-start = (bf16[128,256]{1,0:T(8,128)(2,1)S(1)}, bf16[128,256]{1,0:T(8,128)(2,1)S(1)}, u32[]{:S(2)}, u32[]{:S(2)}) collective-permute-start(bf16[128,256]{1,0:T(8,128)(2,1)S(1)} %broadcast_select_fusion.19), channel_id=1, source_target_pairs={{0,1},{1,2},{2,3},{3,4},{4,5},{5,6},{6,7},{7,8},{8,9},{9,10},{10,1... | collective-permute-start | bytes 196616 | tf_op jit(solution)/shard_map/ppermute | solution.py:15
  18.6 6.4 %collective-permute-start.2 = (bf16[128,256]{1,0:T(8,128)(2,1)S(1)}, bf16[128,256]{1,0:T(8,128)(2,1)S(1)}, u32[]{:S(2)}, u32[]{:S(2)}) collective-permute-start(bf16[128,256]{1,0:T(8,128)(2,1)S(1)} %broadcast_select_fusion.9), channel_id=1, source_target_pairs={{0,16},{1,17},{2,18},{3,19},{4,20},{5,21},{6,22},{7,23},{8,24},{9,... | collective-permute-start | bytes 196616 | tf_op jit(solution)/shard_map/ppermute | solution.py:15
  19.6 6.3 %collective-permute-start.3 = (bf16[128,256]{1,0:T(8,128)(2,1)S(1)}, bf16[128,256]{1,0:T(8,128)(2,1)S(1)}, u32[]{:S(2)}, u32[]{:S(2)}) collective-permute-start(bf16[128,256]{1,0:T(8,128)(2,1)S(1)} %broadcast_select_fusion.4), channel_id=1, source_target_pairs={{0,16},{1,17},{2,18},{3,19},{4,20},{5,21},{6,22},{7,23},{8,24},{9,... | collective-permute-start | bytes 196616 | tf_op jit(solution)/shard_map/ppermute | solution.py:15
  32.5 3.3 %copy-start.1 = (bf16[512,256]{1,0:T(8,128)(2,1)S(1)}, bf16[512,256]{1,0:T(8,128)(2,1)}, u32[]{:S(2)}) copy-start(bf16[512,256]{1,0:T(8,128)(2,1)} %param.15) | copy-start | bytes 786436
  32.5 3.3 %copy-start.2 = (bf16[512,256]{1,0:T(8,128)(2,1)S(1)}, bf16[512,256]{1,0:T(8,128)(2,1)}, u32[]{:S(2)}) copy-start(bf16[512,256]{1,0:T(8,128)(2,1)} %param.13) | copy-start | bytes 786436
  32.5 3.4 %copy-start.3 = (bf16[256,256]{1,0:T(8,128)(2,1)S(1)}, bf16[256,256]{1,0:T(8,128)(2,1)}, u32[]{:S(2)}) copy-start(bf16[256,256]{1,0:T(8,128)(2,1)} %param.16) | copy-start | bytes 393220
  39.8 8.5 %collective-permute-start.4 = (bf16[128,256]{1,0:T(8,128)(2,1)S(1)}, bf16[128,256]{1,0:T(8,128)(2,1)S(1)}, u32[]{:S(2)}, u32[]{:S(2)}) collective-permute-start(bf16[128,256]{1,0:T(8,128)(2,1)S(1)} %broadcast_select_fusion.18), channel_id=1, source_target_pairs={{0,1},{1,2},{2,3},{3,4},{4,5},{5,6},{6,7},{7,8},{8,9},{9,10},{10,1... | collective-permute-start | bytes 196616 | tf_op jit(solution)/shard_map/ppermute | solution.py:15
  39.9 8.3 %collective-permute-start.5 = (bf16[128,256]{1,0:T(8,128)(2,1)S(1)}, bf16[128,256]{1,0:T(8,128)(2,1)S(1)}, u32[]{:S(2)}, u32[]{:S(2)}) collective-permute-start(bf16[128,256]{1,0:T(8,128)(2,1)S(1)} %broadcast_select_fusion.13), channel_id=1, source_target_pairs={{0,31},{1,0},{2,1},{3,2},{4,3},{5,4},{6,5},{7,6},{8,7},{9,8},{10,9... | collective-permute-start | bytes 196616 | tf_op jit(solution)/shard_map/ppermute | solution.py:15
  45.3 5.7 %collective-permute-start.6 = (bf16[128,256]{1,0:T(8,128)(2,1)S(1)}, bf16[128,256]{1,0:T(8,128)(2,1)S(1)}, u32[]{:S(2)}, u32[]{:S(2)}) collective-permute-start(bf16[128,256]{1,0:T(8,128)(2,1)S(1)} %broadcast_select_fusion.8), channel_id=1, source_target_pairs={{0,16},{1,17},{2,18},{3,19},{4,20},{5,21},{6,22},{7,23},{8,24},{9,... | collective-permute-start | bytes 196616 | tf_op jit(solution)/shard_map/ppermute | solution.py:15
  45.4 6.4 %collective-permute-start.7 = (bf16[128,256]{1,0:T(8,128)(2,1)S(1)}, bf16[128,256]{1,0:T(8,128)(2,1)S(1)}, u32[]{:S(2)}, u32[]{:S(2)}) collective-permute-start(bf16[128,256]{1,0:T(8,128)(2,1)S(1)} %broadcast_select_fusion.3), channel_id=1, source_target_pairs={{0,16},{1,17},{2,18},{3,19},{4,20},{5,21},{6,22},{7,23},{8,24},{9,... | collective-permute-start | bytes 196616 | tf_op jit(solution)/shard_map/ppermute | solution.py:15
  68.1 8.6 %collective-permute-start.8 = (bf16[128,256]{1,0:T(8,128)(2,1)S(1)}, bf16[128,256]{1,0:T(8,128)(2,1)S(1)}, u32[]{:S(2)}, u32[]{:S(2)}) collective-permute-start(bf16[128,256]{1,0:T(8,128)(2,1)S(1)} %broadcast_select_fusion.17), channel_id=1, source_target_pairs={{0,1},{1,2},{2,3},{3,4},{4,5},{5,6},{6,7},{7,8},{8,9},{9,10},{10,1... | collective-permute-start | bytes 196616 | tf_op jit(solution)/shard_map/ppermute | solution.py:15
  68.3 8.5 %collective-permute-start.9 = (bf16[128,256]{1,0:T(8,128)(2,1)S(1)}, bf16[128,256]{1,0:T(8,128)(2,1)S(1)}, u32[]{:S(2)}, u32[]{:S(2)}) collective-permute-start(bf16[128,256]{1,0:T(8,128)(2,1)S(1)} %broadcast_select_fusion.12), channel_id=1, source_target_pairs={{0,31},{1,0},{2,1},{3,2},{4,3},{5,4},{6,5},{7,6},{8,7},{9,8},{10,9... | collective-permute-start | bytes 196616 | tf_op jit(solution)/shard_map/ppermute | solution.py:15
  73.9 5.2 %collective-permute-start.10 = (bf16[128,256]{1,0:T(8,128)(2,1)S(1)}, bf16[128,256]{1,0:T(8,128)(2,1)S(1)}, u32[]{:S(2)}, u32[]{:S(2)}) collective-permute-start(bf16[128,256]{1,0:T(8,128)(2,1)S(1)} %broadcast_select_fusion.7), channel_id=1, source_target_pairs={{0,16},{1,17},{2,18},{3,19},{4,20},{5,21},{6,22},{7,23},{8,24},{9,... | collective-permute-start | bytes 196616 | tf_op jit(solution)/shard_map/ppermute | solution.py:15
  73.9 5.9 %collective-permute-start.11 = (bf16[128,256]{1,0:T(8,128)(2,1)S(1)}, bf16[128,256]{1,0:T(8,128)(2,1)S(1)}, u32[]{:S(2)}, u32[]{:S(2)}) collective-permute-start(bf16[128,256]{1,0:T(8,128)(2,1)S(1)} %broadcast_select_fusion.2), channel_id=1, source_target_pairs={{0,16},{1,17},{2,18},{3,19},{4,20},{5,21},{6,22},{7,23},{8,24},{9,... | collective-permute-start | bytes 196616 | tf_op jit(solution)/shard_map/ppermute | solution.py:15
  96.1 8.5 %collective-permute-start.12 = (bf16[128,256]{1,0:T(8,128)(2,1)S(1)}, bf16[128,256]{1,0:T(8,128)(2,1)S(1)}, u32[]{:S(2)}, u32[]{:S(2)}) collective-permute-start(bf16[128,256]{1,0:T(8,128)(2,1)S(1)} %broadcast_select_fusion.16), channel_id=1, source_target_pairs={{0,1},{1,2},{2,3},{3,4},{4,5},{5,6},{6,7},{7,8},{8,9},{9,10},{10,1... | collective-permute-start | bytes 196616 | tf_op jit(solution)/shard_map/ppermute | solution.py:15
  96.2 8.3 %collective-permute-start.13 = (bf16[128,256]{1,0:T(8,128)(2,1)S(1)}, bf16[128,256]{1,0:T(8,128)(2,1)S(1)}, u32[]{:S(2)}, u32[]{:S(2)}) collective-permute-start(bf16[128,256]{1,0:T(8,128)(2,1)S(1)} %broadcast_select_fusion.11), channel_id=1, source_target_pairs={{0,31},{1,0},{2,1},{3,2},{4,3},{5,4},{6,5},{7,6},{8,7},{9,8},{10,9... | collective-permute-start | bytes 196616 | tf_op jit(solution)/shard_map/ppermute | solution.py:15
  101.6 5.2 %collective-permute-start.14 = (bf16[128,256]{1,0:T(8,128)(2,1)S(1)}, bf16[128,256]{1,0:T(8,128)(2,1)S(1)}, u32[]{:S(2)}, u32[]{:S(2)}) collective-permute-start(bf16[128,256]{1,0:T(8,128)(2,1)S(1)} %broadcast_select_fusion.6), channel_id=1, source_target_pairs={{0,16},{1,17},{2,18},{3,19},{4,20},{5,21},{6,22},{7,23},{8,24},{9,... | collective-permute-start | bytes 196616 | tf_op jit(solution)/shard_map/ppermute | solution.py:15
  102.1 5.4 %collective-permute-start.15 = (bf16[128,256]{1,0:T(8,128)(2,1)S(1)}, bf16[128,256]{1,0:T(8,128)(2,1)S(1)}, u32[]{:S(2)}, u32[]{:S(2)}) collective-permute-start(bf16[128,256]{1,0:T(8,128)(2,1)S(1)} %broadcast_select_fusion.1), channel_id=1, source_target_pairs={{0,16},{1,17},{2,18},{3,19},{4,20},{5,21},{6,22},{7,23},{8,24},{9,... | collective-permute-start | bytes 196616 | tf_op jit(solution)/shard_map/ppermute | solution.py:15
  124.6 8.7 %collective-permute-start.16 = (bf16[128,256]{1,0:T(8,128)(2,1)S(1)}, bf16[128,256]{1,0:T(8,128)(2,1)S(1)}, u32[]{:S(2)}, u32[]{:S(2)}) collective-permute-start(bf16[128,256]{1,0:T(8,128)(2,1)S(1)} %broadcast_select_fusion.15), channel_id=1, source_target_pairs={{0,1},{1,2},{2,3},{3,4},{4,5},{5,6},{6,7},{7,8},{8,9},{9,10},{10,1... | collective-permute-start | bytes 196616 | tf_op jit(solution)/shard_map/ppermute | solution.py:15
  124.8 8.5 %collective-permute-start.17 = (bf16[128,256]{1,0:T(8,128)(2,1)S(1)}, bf16[128,256]{1,0:T(8,128)(2,1)S(1)}, u32[]{:S(2)}, u32[]{:S(2)}) collective-permute-start(bf16[128,256]{1,0:T(8,128)(2,1)S(1)} %broadcast_select_fusion.10), channel_id=1, source_target_pairs={{0,31},{1,0},{2,1},{3,2},{4,3},{5,4},{6,5},{7,6},{8,7},{9,8},{10,9... | collective-permute-start | bytes 196616 | tf_op jit(solution)/shard_map/ppermute | solution.py:15
  130.4 5.2 %collective-permute-start.18 = (bf16[128,256]{1,0:T(8,128)(2,1)S(1)}, bf16[128,256]{1,0:T(8,128)(2,1)S(1)}, u32[]{:S(2)}, u32[]{:S(2)}) collective-permute-start(bf16[128,256]{1,0:T(8,128)(2,1)S(1)} %broadcast_select_fusion.5), channel_id=1, source_target_pairs={{0,16},{1,17},{2,18},{3,19},{4,20},{5,21},{6,22},{7,23},{8,24},{9,... | collective-permute-start | bytes 196616 | tf_op jit(solution)/shard_map/ppermute | solution.py:15
  130.8 5.4 %collective-permute-start.19 = (bf16[128,256]{1,0:T(8,128)(2,1)S(1)}, bf16[128,256]{1,0:T(8,128)(2,1)S(1)}, u32[]{:S(2)}, u32[]{:S(2)}) collective-permute-start(bf16[128,256]{1,0:T(8,128)(2,1)S(1)} %broadcast_select_fusion), channel_id=1, source_target_pairs={{0,16},{1,17},{2,18},{3,19},{4,20},{5,21},{6,22},{7,23},{8,24},{9,... | collective-permute-start | bytes 196616 | tf_op jit(solution)/shard_map/ppermute | solution.py:15
  145.4 3.5 %copy-start.4 = (bf16[512,256]{1,0:T(8,128)(2,1)S(1)}, bf16[512,256]{1,0:T(8,128)(2,1)}, u32[]{:S(2)}) copy-start(bf16[512,256]{1,0:T(8,128)(2,1)} %param.14) | copy-start | bytes 786436
Sparse Core Ops, SparseCore 0:
  150.4 124.5 all-reduce.1
where the time goes:
time: 284 us
  waiting for transfers between devices  139 us (49%)
  local copies, waits for them, and re-layouts  45.8 us (16%)
  starting transfers between devices  43.4 us (15%)
  matrix products  35.9 us (13%)
  between operations  15.2 us (5%)
  other arithmetic  3.69 us (1%)
    psum x1, waiting for transfers between devices, per_device(): lax.psum(lax.dot_general(state_values, final_mixed, (((0,), (0,)), ((), (...  125 us
    ppermute x20, starting transfers between devices, passed_along(): return lax.ppermute(value, axis, pairs)  43.4 us
    unnamed x35, local copies, waits for them, and re-layouts  19.7 us
    dot_general x5, matrix products, add_tiles(): jnp.einsum('tij,tjh->tih', tiles, rows, preferred_element_type=jnp.float32)  17.2 us
    gather x20, local copies, waits for them, and re-layouts, with_boundary(): chosen = jnp.take(scaled, send_rows[direction], axis=0)  16.9 us
    dot_general x5, matrix products, add_tiles(): jnp.dot(onehot, prod.reshape(slots, size * width), precision=lax.Precisio...  15.5 us
    ppermute x20, waiting for transfers between devices, passed_along(): return lax.ppermute(value, axis, pairs)  14.8 us
    gather x5, local copies, waits for them, and re-layouts, add_tiles(): rows = jnp.take(stacked, index, axis=0)  8.06 us
  transfers between devices with their start and end apart: 21, of which 11 were waited for; matrix products, arithmetic and copies ran while one was open for 1% of the time, Pallas kernels for 0%

commit v1 on v0

v1 whole, which is shorter than its diff:
```python
import functools

import jax
import jax.numpy as jnp
from jax import lax
from jax.experimental import pallas as pl
from jax.experimental.pallas import tpu as pltpu
from jax.sharding import PartitionSpec as P

ITERS = 4
REACH = 16
LISTS = 4
BF = jnp.bfloat16
F32 = jnp.float32
VMEM_BYTES = 24 * 1024 * 1024


def call(body, outs, ins, scratch=()):
    spaces = {"v": pltpu.VMEM, "s": pltpu.SMEM}
    return pl.pallas_call(
        body,
        out_shape=tuple(jax.ShapeDtypeStruct(shape, dtype) for shape, dtype in outs),
        in_specs=[pl.BlockSpec(memory_space=spaces[kind]) for kind in ins],
        out_specs=tuple(pl.BlockSpec(memory_space=pltpu.VMEM) for _ in outs),
        scratch_shapes=list(scratch),
        compiler_params=pltpu.CompilerParams(vmem_limit_bytes=VMEM_BYTES),
    )


def mm(a, b):
    return jnp.dot(a, b, preferred_element_type=F32)


def mm_rhs_t(a, b):
    return lax.dot_general(a, b, (((1,), (1,)), ((), ())), preferred_element_type=F32)


def mm_lhs_t(a, b):
    return lax.dot_general(a, b, (((0,), (0,)), ((), ())), preferred_element_type=F32)


def first_body(parity, lists, grad, slopes, scaled, pick, near, far, wide):
    size = lists.shape[1]
    rows = grad.shape[0]
    odd = parity[0] == 1
    order = (
        jnp.where(odd, lists[1:2, :], lists[0:1, :]),
        jnp.where(odd, lists[0:1, :], lists[1:2, :]),
        lists[2:3, :],
        lists[3:4, :],
    )
    column = lax.broadcasted_iota(jnp.int32, (size, rows), 1)
    for n in range(LISTS):
        wanted = jnp.broadcast_to(order[n], (size, size)).astype(F32).T.astype(jnp.int32)
        wanted = jnp.concatenate([wanted] * (rows // size), axis=1)
        pick[n * size : (n + 1) * size, :] = (wanted == column).astype(F32).astype(BF)
    value = (slopes[...].astype(F32) * grad[...].astype(F32)).astype(BF)
    scaled[...] = value
    sent = mm(pick[...], value).astype(BF)
    near[...] = sent[:size]
    far[...] = sent[size : 2 * size]
    wide[...] = sent[2 * size :]


def setup_body(
    parity, dst, src, count, tiles, pick, grad, slopes, scaled, states,
    own, edge, pick_own, pick_edge, pick_grad, pick_slopes, local, pick_local,
    back_own, back_near, back_far, back_wide, total,
):
    size = tiles.shape[1]
    blocks = total.shape[0]
    half = blocks // 2
    total[...] = jnp.zeros_like(total)
    even = parity[0] == 0

    def add(slot, carry):
        source = src[slot]
        swapped = even & ((source == half) | (source == half + 1))
        source = jnp.where(swapped, 2 * half + 1 - source, source)
        at = pl.ds(pl.multiple_of(dst[slot] * size, size), size)
        total[source, at, :] = total[source, at, :] + tiles[slot].astype(F32)
        return carry

    lax.fori_loop(0, count[0], add, 0)
    for b in range(half):
        at = slice(b * size, (b + 1) * size)
        own[:, at] = total[b].astype(BF)
        edge[:, at] = total[half + b].astype(BF)
    chosen = pick[...]
    pick_own[...] = mm(chosen, own[...]).astype(BF)
    pick_edge[...] = mm(chosen, edge[...]).astype(BF)
    pick_grad[...] = mm(chosen, grad[...]).astype(BF)
    pick_slopes[...] = mm(chosen, slopes[...]).astype(BF)
    local[...] = mm(own[...], scaled[...])
    pick_local[...] = mm(pick_own[...], scaled[...])
    back_own[...] = mm_lhs_t(own[...], states[...])
    back = mm_lhs_t(edge[...], states[...]).astype(BF)
    back_near[...] = back[:size]
    back_far[...] = back[size : 2 * size]
    back_wide[...] = back[2 * size :]


def send_body(near, far, wide, pick_local, pick_edge, pick_grad, pick_slopes, weight, near_out, far_out, wide_out):
    size = near.shape[0]
    came = jnp.concatenate([near[...], far[...], wide[...]], axis=0)
    mixed = (pick_local[...] + mm(pick_edge[...], came)).astype(BF)
    adjoint = pick_grad[...].astype(F32) + mm_rhs_t(mixed, weight[...])
    sent = (pick_slopes[...].astype(F32) * adjoint).astype(BF)
    near_out[...] = sent[:size]
    far_out[...] = sent[size : 2 * size]
    wide_out[...] = sent[2 * size :]


def own_body(near, far, wide, local, edge, grad, slopes, weight, own, pick_own, local_out, pick_local_out):
    came = jnp.concatenate([near[...], far[...], wide[...]], axis=0)
    mixed = (local[...] + mm(edge[...], came)).astype(BF)
    adjoint = grad[...].astype(F32) + mm_rhs_t(mixed, weight[...])
    scaled = (slopes[...].astype(F32) * adjoint).astype(BF)
    local_out[...] = mm(own[...], scaled)
    pick_local_out[...] = mm(pick_own[...], scaled)


def back_body(near, far, wide, back_own, pick, high, low):
    came = jnp.concatenate([near[...], far[...], wide[...]], axis=0)
    value = (back_own[...] + mm_lhs_t(pick[...], came)).T
    top = value.astype(BF)
    high[...] = top
    low[...] = (value - top.astype(F32)).astype(BF)


def last_body(factor, near, far, wide, local, edge, grad, slopes, weight, high, low, adjoint_out, partial):
    came = jnp.concatenate([near[...], far[...], wide[...]], axis=0)
    mixed = (local[...] + mm(edge[...], came)).astype(BF)
    adjoint = grad[...].astype(F32) + mm_rhs_t(mixed, weight[...])
    adjoint_out[...] = adjoint
    scaled = (slopes[...].astype(F32) * adjoint).astype(BF)
    partial[...] = (mm(high[...], scaled) + mm(low[...], scaled)) * factor


def exchange(near, far, wide, forward):
    count = lax.axis_size("dom")
    everyone = range(count)
    size = near.shape[0]
    ahead = [(p, (p + REACH) % count) for p in everyone]
    behind = [(p, (p - REACH) % count) for p in everyone]
    if not forward:
        ahead, behind = behind, ahead
    if ahead == behind:
        wide = lax.ppermute(wide, "dom", ahead)
    else:
        wide = jnp.concatenate(
            [lax.ppermute(wide[:size], "dom", ahead), lax.ppermute(wide[size:], "dom", behind)], axis=0
        )
    far = lax.ppermute(far, "dom", [(p, (p + 1 if p % 2 else p - 1) % count) for p in everyone])
    near = lax.ppermute(near, "dom", [(p, p ^ 1) for p in everyone])
    return near, far, wide


def summed(partial, parity):
    count = lax.axis_size("dom")
    if count & (count - 1):
        return lax.psum(partial, "dom")
    total = partial + lax.ppermute(partial, "dom", [(p, p + 1) for p in range(0, count, 2)])
    step = 2
    while step < count:
        mine = total.astype(BF)
        total = mine.astype(F32) + lax.ppermute(
            mine, "dom", [(p, p ^ step) for p in range(1, count, 2)]
        ).astype(F32)
        step *= 2
    theirs = lax.ppermute(total, "dom", [(p, p - 1) for p in range(1, count, 2)])
    return jnp.where(parity == 1, total, theirs)


def per_device(grad_out, states, slopes, weight, tiles, tile_dst, tile_src, tile_count, send_rows):
    rows, width = grad_out.shape
    slots, size, _ = tiles.shape
    cut = LISTS * size
    blocks = rows // size + LISTS
    parity = (lax.axis_index("dom") % 2).astype(jnp.int32).reshape(1)
    message = [((size, width), BF), ((size, width), BF), ((2 * size, width), BF)]

    scaled, pick, near, far, wide = call(
        first_body, [((rows, width), BF), ((cut, rows), BF)] + message, "svvv"
    )(parity, send_rows, grad_out, slopes)
    came = exchange(near, far, wide, True)
    (
        own, edge, pick_own, pick_edge, pick_grad, pick_slopes, local, pick_local, back_own, *back
    ) = call(
        setup_body,
        [
            ((rows, rows), BF), ((rows, cut), BF), ((cut, rows), BF), ((cut, cut), BF),
            ((cut, width), BF), ((cut, width), BF), ((rows, width), F32), ((cut, width), F32),
            ((rows, width), F32),
        ] + message,
        "ssssvvvvvv",
        [pltpu.VMEM((blocks, rows, size), F32)],
    )(parity, tile_dst, tile_src, tile_count, tiles, pick, grad_out, slopes, scaled, states)
    back_came = exchange(*back, False)
    high, low = call(back_body, [((width, rows), BF), ((width, rows), BF)], "vvvvv")(*back_came, back_own, pick)

    for step in range(ITERS - 1):
        sent = call(send_body, message, "v" * 8)(*came, pick_local, pick_edge, pick_grad, pick_slopes, weight)
        local_next = call(own_body, [((rows, width), F32), ((cut, width), F32)], "v" * 10)(
            *came, local, edge, grad_out, slopes, weight, own, pick_own
        )
        came = exchange(*sent, True)
        local, pick_local = local_next
    factor = 1.0 / float(lax.axis_size("dom") * rows) ** 0.5
    adjoint, partial = call(
        functools.partial(last_body, factor), [((rows, width), F32), ((width, width), F32)], "v" * 10
    )(*came, local, edge, grad_out, slopes, weight, high, low)
    return adjoint, summed(partial, parity[0])


def solution(mesh):
    in_specs = (
        P("dom", None),
        P("dom", None),
        P("dom", None),
        P(),
        P("dom", None, None),
        P("dom"),
        P("dom"),
        P("dom"),
        P("dom", None),
    )
    out_specs = (P("dom", None), P())
    return jax.shard_map(
        per_device, mesh=mesh, in_specs=in_specs, out_specs=out_specs, check_vma=False
    )
```

time: 284 us -> 84.4 us (0.30)
  waiting for transfers between devices: 139 us -> 36.1 us
  local copies, waits for them, and re-layouts: 45.8 us -> 5.3 us
  matrix products: 35.9 us -> 0 us
  between operations: 15.2 us -> 1.57 us
  starting transfers between devices: 43.4 us -> 30.7 us
  Pallas kernels: 0 us -> 9.45 us
    psum x1 -> x0, waiting for transfers between devices: 125 us -> none  [per_device(): lax.psum(lax.dot_general(state_values, final_mixed, (((0,), (0,)), ((), (...]
    dot_general x15 -> x0, matrix products: 35.9 us -> none  [the longest x5 17.2 us: add_tiles(): jnp.einsum('tij,tjh->tih', tiles, rows, preferred_element_type=jnp.float32)]
    gather x25 -> x0, local copies, waits for them, and re-layouts: 25 us -> none  [the longest x20 16.9 us: with_boundary(): chosen = jnp.take(scaled, send_rows[direction], axis=0)]
    ppermute x20 -> x21, waiting for transfers between devices: 14.8 us -> 36.1 us  [the longest x1 23.5 us: summed(): lax.ppermute(total, 'dom', [(p, p - 1) for p in range(1, count, 2)])]
    unnamed x35 -> x20, local copies, waits for them, and re-layouts: 19.7 us -> 5.3 us
    ppermute x20 -> x21, starting transfers between devices: 43.4 us -> 30.7 us  [the longest x5 14 us: exchange(): wide = lax.ppermute(wide, 'dom', ahead)]
    pallas_call x0 -> x10, Pallas kernels: none -> 9.45 us  [the longest x3 3.31 us: per_device(): call(own_body, [((rows, width), F32), ((cut, width), F32)], 'v' * 10)]
  transfers between devices with their start and end apart: 21 -> 21, of which waited for: 11 -> 5; matrix products, arithmetic and copies ran while one was open for 1% -> 0% of each run, Pallas kernels for 0% -> 8%
where the time goes in v1:
time: 84.4 us; the launch traced here: 84 us
  waiting for transfers between devices  36.1 us (43%)
  starting transfers between devices  30.7 us (36%)
  Pallas kernels  9.45 us (11%)
  local copies, waits for them, and re-layouts  5.3 us (6%)
  between operations  1.57 us (2%)
  other arithmetic  0.92 us (1%)
    ppermute x1, waiting for transfers between devices, summed(): lax.ppermute(total, 'dom', [(p, p - 1) for p in range(1, count, 2)])  23.5 us
    ppermute x5, starting transfers between devices, exchange(): wide = lax.ppermute(wide, 'dom', ahead)  14 us
    ppermute x5, waiting for transfers between devices, exchange(): lax.ppermute(far, 'dom', [(p, (p + 1 if p % 2 else p - 1) % count) for p...  11.4 us
    ppermute x5, starting transfers between devices, exchange(): lax.ppermute(far, 'dom', [(p, (p + 1 if p % 2 else p - 1) % count) for p...  11.4 us
    unnamed x20, local copies, waits for them, and re-layouts  5.3 us
    pallas_call x3, Pallas kernels, per_device(): call(own_body, [((rows, width), F32), ((cut, width), F32)], 'v' * 10)  3.31 us
    ppermute x4, starting transfers between devices, summed(): lax.ppermute(mine, 'dom', [(p, p ^ step) for p in range(1, count, 2)])  2.68 us
    pallas_call x1, Pallas kernels, per_device(): call(setup_body, [((rows, rows), BF), ((rows, cut), BF), ((cut, rows), BF...  2.51 us
  transfers between devices with their start and end apart: 21, of which 5 were waited for; matrix products, arithmetic and copies ran while one was open for 0% of the time, Pallas kernels for 8%

profile of v1, /device:TPU:0, one launch (start us, length us, event | category | flops | bytes accessed | tf_op | source)
XLA Modules:
  0.0 84.0 jit_solution(13389113444643452992)
XLA Ops:
  0.7 0.7 copy-done.7
  1.3 0.9 %copy-done = bf16[512,256]{1,0:T(8,128)(2,1)S(1)} copy-done((bf16[512,256]{1,0:T(8,128)(2,1)S(1)}, bf16[512,256]{1,0:T(8,128)(2,1)}, u32[]{:S(2)}) %copy-start) | copy-done | bytes 262168
  2.3 0.9 %copy-done.2 = bf16[512,256]{1,0:T(8,128)(2,1)S(1)} copy-done((bf16[512,256]{1,0:T(8,128)(2,1)S(1)}, bf16[512,256]{1,0:T(8,128)(2,1)}, u32[]{:S(2)}) %copy-start.2) | copy-done | bytes 262168
  3.2 0.4 shard_map.104
  3.6 4.1 %collective-permute-start.2 = (bf16[256,256]{1,0:T(8,128)(2,1)S(1)}, bf16[256,256]{1,0:T(8,128)(2,1)S(1)}, u32[]{:S(2)}, u32[]{:S(2)}) collective-permute-start(bf16[256,256]{1,0:T(8,128)(2,1)S(1)} %get-tuple-element.39), channel_id=1, source_target_pairs={{0,16},{1,17},{2,18},{3,19},{4,20},{5,21},{6,22},{7,23},{8,24},{9,... | collective-permute-start | bytes 393224 | tf_op jit(solution)/shard_map/ppermute | solution.py:149
  7.7 3.3 %collective-permute-start.1 = (bf16[128,256]{1,0:T(8,128)(2,1)S(1)}, bf16[128,256]{1,0:T(8,128)(2,1)S(1)}, u32[]{:S(2)}, u32[]{:S(2)}) collective-permute-start(bf16[128,256]{1,0:T(8,128)(2,1)S(1)} %get-tuple-element.38), channel_id=1, source_target_pairs={{0,31},{1,2},{2,1},{3,4},{4,3},{5,6},{6,5},{7,8},{8,7},{9,10},{10,... | collective-permute-start | bytes 196616 | tf_op jit(solution)/shard_map/ppermute | solution.py:154
  11.7 0.0 copy-start.8
  11.8 0.0 copy-start.9
  11.8 0.6 copy-done.8
  12.4 0.0 copy-done.9
  12.4 1.1 %copy-done.5 = bf16[24,128,128]{2,1,0:T(8,128)(2,1)S(1)} copy-done((bf16[24,128,128]{2,1,0:T(8,128)(2,1)S(1)}, bf16[24,128,128]{2,1,0:T(8,128)(2,1)}, u32[]{:S(2)}) %copy-start.5) | copy-done | bytes 786456
  13.6 0.9 %copy-done.6 = bf16[512,256]{1,0:T(8,128)(2,1)S(1)} copy-done((bf16[512,256]{1,0:T(8,128)(2,1)S(1)}, bf16[512,256]{1,0:T(8,128)(2,1)}, u32[]{:S(2)}) %copy-start.6) | copy-done | bytes 262168
  14.5 2.5 %shard_map.105 = (bf16[512,512]{1,0:T(8,128)(2,1)S(1)}, bf16[512,512]{1,0:T(8,128)(2,1)S(1)}, bf16[512,512]{1,0:T(8,128)(2,1)S(1)}, bf16[512,512]{1,0:T(8,128)(2...) custom-call(s32[1]{0:T(128)} %bitcast.parity, ...), custom_call_target="tpu_custom_call" | custom-call | tf_op jit(solution)/shard_map/pallas_call | solution.py:189
  17.0 0.0 collective-permute-done.near
  17.1 0.5 shard_map.106
  17.6 2.3 %collective-permute-start.5 = (bf16[256,256]{1,0:T(8,128)(2,1)S(1)}, bf16[256,256]{1,0:T(8,128)(2,1)S(1)}, u32[]{:S(2)}, u32[]{:S(2)}) collective-permute-start(bf16[256,256]{1,0:T(8,128)(2,1)S(1)} %get-tuple-element.48), channel_id=1, source_target_pairs={{0,16},{1,17},{2,18},{3,19},{4,20},{5,21},{6,22},{7,23},{8,24},{9,... | collective-permute-start | bytes 393224 | tf_op jit(solution)/shard_map/ppermute | solution.py:149
  19.8 0.0 collective-permute-start.3
  19.9 1.0 %collective-permute-start.4 = (bf16[128,256]{1,0:T(8,128)(2,1)S(1)}, bf16[128,256]{1,0:T(8,128)(2,1)S(1)}, u32[]{:S(2)}, u32[]{:S(2)}) collective-permute-start(bf16[128,256]{1,0:T(8,128)(2,1)S(1)} %get-tuple-element.47), channel_id=1, source_target_pairs={{0,31},{1,2},{2,1},{3,4},{4,3},{5,6},{6,5},{7,8},{8,7},{9,10},{10,... | collective-permute-start | bytes 196616 | tf_op jit(solution)/shard_map/ppermute | solution.py:154
  20.9 0.8 shard_map.107
  21.7 0.0 collective-permute-done.3.near
  21.7 5.5 %collective-permute-done.4.far = bf16[128,256]{1,0:T(8,128)(2,1)S(1)} collective-permute-done((bf16[128,256]{1,0:T(8,128)(2,1)S(1)}, bf16[128,256]{1,0:T(8,128)(2,1)S(1)}, u32[]{:S(2)}, u32[]{:S(2)}) %collective-permute-start.4) | collective-permute-done | bytes 65568 | tf_op jit(solution)/shard_map/ppermute | solution.py:154
  27.2 0.0 collective-permute-done.5.wide
  27.2 0.5 shard_map.108
  27.7 0.8 collective-permute-start.8
  28.6 0.0 collective-permute-start.6
  28.6 1.7 %collective-permute-start.7 = (bf16[128,256]{1,0:T(8,128)(2,1)S(1)}, bf16[128,256]{1,0:T(8,128)(2,1)S(1)}, u32[]{:S(2)}, u32[]{:S(2)}) collective-permute-start(bf16[128,256]{1,0:T(8,128)(2,1)S(1)} %get-tuple-element.55), channel_id=1, source_target_pairs={{0,31},{1,2},{2,1},{3,4},{4,3},{5,6},{6,5},{7,8},{8,7},{9,10},{10,... | collective-permute-start | bytes 196616 | tf_op jit(solution)/shard_map/ppermute | solution.py:154
  30.3 0.0 collective-permute-start.12
  30.3 1.0 %collective-permute-start.14 = (bf16[256,256]{1,0:T(8,128)(2,1)S(1)}, bf16[256,256]{1,0:T(8,128)(2,1)S(1)}, u32[]{:S(2)}, u32[]{:S(2)}) collective-permute-start(bf16[256,256]{1,0:T(8,128)(2,1)S(1)} %get-tuple-element.66), channel_id=1, source_target_pairs={{0,16},{1,17},{2,18},{3,19},{4,20},{5,21},{6,22},{7,23},{8,24},{9,... | collective-permute-start | bytes 393224 | tf_op jit(solution)/shard_map/ppermute | solution.py:149
  31.2 0.8 shard_map.109
  32.1 3.9 %collective-permute-done.7.far = bf16[128,256]{1,0:T(8,128)(2,1)S(1)} collective-permute-done((bf16[128,256]{1,0:T(8,128)(2,1)S(1)}, bf16[128,256]{1,0:T(8,128)(2,1)S(1)}, u32[]{:S(2)}, u32[]{:S(2)}) %collective-permute-start.7) | collective-permute-done | bytes 65568 | tf_op jit(solution)/shard_map/ppermute | solution.py:154
  36.0 0.5 shard_map.110
  36.5 5.8 %collective-permute-start.11 = (bf16[256,256]{1,0:T(8,128)(2,1)S(1)}, bf16[256,256]{1,0:T(8,128)(2,1)S(1)}, u32[]{:S(2)}, u32[]{:S(2)}) collective-permute-start(bf16[256,256]{1,0:T(8,128)(2,1)S(1)} %get-tuple-element.61), channel_id=1, source_target_pairs={{0,16},{1,17},{2,18},{3,19},{4,20},{5,21},{6,22},{7,23},{8,24},{9,... | collective-permute-start | bytes 393224 | tf_op jit(solution)/shard_map/ppermute | solution.py:149
  42.3 0.0 collective-permute-start.9
  42.3 0.0 collective-permute-done.12.near
  42.3 5.3 %collective-permute-start.10 = (bf16[128,256]{1,0:T(8,128)(2,1)S(1)}, bf16[128,256]{1,0:T(8,128)(2,1)S(1)}, u32[]{:S(2)}, u32[]{:S(2)}) collective-permute-start(bf16[128,256]{1,0:T(8,128)(2,1)S(1)} %get-tuple-element.60), channel_id=1, source_target_pairs={{0,31},{1,2},{2,1},{3,4},{4,3},{5,6},{6,5},{7,8},{8,7},{9,10},{10,... | collective-permute-start | bytes 196616 | tf_op jit(solution)/shard_map/ppermute | solution.py:154
  47.6 2.0 %collective-permute-done.13.far = bf16[128,256]{1,0:T(8,128)(2,1)S(1)} collective-permute-done((bf16[128,256]{1,0:T(8,128)(2,1)S(1)}, bf16[128,256]{1,0:T(8,128)(2,1)S(1)}, u32[]{:S(2)}, u32[]{:S(2)}) %collective-permute-start.13) | collective-permute-done | bytes 65568 | tf_op jit(solution)/shard_map/ppermute | solution.py:154
  49.6 0.4 shard_map.112
  50.1 1.6 %shard_map.111 = (f32[512,256]{1,0:T(8,128)S(1)}, f32[512,256]{1,0:T(8,128)}) custom-call(bf16[128,256]{1,0:T(8,128)(2,1)S(1)} %collective-permute-done.6.near, bf16[128,256]{1,0:T(8,128)(2,1)S(1)} %collective-permute-done.7.far, bf16[256,256]{1,0:T(8,128)(2,1)S(1)} %collective-permute-done.8.wide, f32[512,256]{1,0:T(8,128)S(1)} %get-tuple-element.62.local, ...), custom_call_target="tpu_custom_call" | custom-call | tf_op jit(solution)/shard_map/pallas_call | solution.py:204
  51.7 1.3 %shard_map.113 = (f32[512,256]{1,0:T(8,128)}, f32[256,256]{1,0:T(8,128)S(1)}) custom-call(bf16[128,256]{1,0:T(8,128)(2,1)S(1)} %collective-permute-done.9.near, bf16[128,256]{1,0:T(8,128)(2,1)S(1)} %collective-permute-done.10.far, bf16[256,256]{1,0:T(8,128)(2,1)S(1)} %collective-permute-done.11.wide, f32[512,256]{1,0:T(8,128)S(1)} %get-tuple-element.63.local, ...), custom_call_target="tpu_custom_call" | custom-call | tf_op jit(solution)/shard_map/pallas_call | solution.py:210
  53.1 1.3 %collective-permute-start.15 = (f32[256,256]{1,0:T(8,128)S(1)}, f32[256,256]{1,0:T(8,128)S(1)}, u32[]{:S(2)}, u32[]{:S(2)}) collective-permute-start(f32[256,256]{1,0:T(8,128)S(1)} %get-tuple-element.71), channel_id=1, source_target_pairs={{0,1},{2,3},{4,5},{6,7},{8,9},{10,11},{12,13},{14,15},{16,17},{18,... | collective-permute-start | bytes 786440 | tf_op jit(solution)/shard_map/ppermute | solution.py:163
  54.4 1.1 %collective-permute-done.15 = f32[256,256]{1,0:T(8,128)S(1)} collective-permute-done((f32[256,256]{1,0:T(8,128)S(1)}, f32[256,256]{1,0:T(8,128)S(1)}, u32[]{:S(2)}, u32[]{:S(2)}) %collective-permute-start.15) | collective-permute-done | bytes 262176 | tf_op jit(solution)/shard_map/ppermute | solution.py:163
  55.5 0.7 collective-permute-start.16
  56.3 0.7 collective-permute-start.17
  57.0 0.7 collective-permute-start.18
  57.7 0.7 collective-permute-start.19
  58.5 1.3 %collective-permute-start.20 = (f32[256,256]{1,0:T(8,128)S(1)}, f32[256,256]{1,0:T(8,128)S(1)}, u32[]{:S(2)}, u32[]{:S(2)}) collective-permute-start(f32[256,256]{1,0:T(8,128)S(1)} %convert_add_fusion), channel_id=1, source_target_pairs={{1,0},{3,2},{5,4},{7,6},{9,8},{11,10},{13,12},{15,14},{17,16},{19,... | collective-permute-start | bytes 786440 | tf_op jit(solution)/shard_map/ppermute | solution.py:171
  59.8 23.5 %collective-permute-done.20 = f32[256,256]{1,0:T(8,128)S(1)} collective-permute-done((f32[256,256]{1,0:T(8,128)S(1)}, f32[256,256]{1,0:T(8,128)S(1)}, u32[]{:S(2)}, u32[]{:S(2)}) %collective-permute-start.20) | collective-permute-done | bytes 262176 | tf_op jit(solution)/shard_map/ppermute | solution.py:171
  83.2 0.7 broadcast_select_fusion
  (30 shorter events, 0.2 us)
Async XLA Ops:
  0.6 0.7 copy-start.7
  1.3 0.9 %copy-start = (bf16[512,256]{1,0:T(8,128)(2,1)S(1)}, bf16[512,256]{1,0:T(8,128)(2,1)}, u32[]{:S(2)}) copy-start(bf16[512,256]{1,0:T(8,128)(2,1)} %grad.11) | copy-start | bytes 786436
  2.3 0.9 %copy-start.2 = (bf16[512,256]{1,0:T(8,128)(2,1)S(1)}, bf16[512,256]{1,0:T(8,128)(2,1)}, u32[]{:S(2)}) copy-start(bf16[512,256]{1,0:T(8,128)(2,1)} %slopes.11) | copy-start | bytes 786436
  3.2 8.5 %copy-start.1 = (bf16[512,256]{1,0:T(8,128)(2,1)S(1)}, bf16[512,256]{1,0:T(8,128)(2,1)}, u32[]{:S(2)}) copy-start(bf16[512,256]{1,0:T(8,128)(2,1)} %grad.11) | copy-start | bytes 786436
  3.2 8.6 %copy-start.3 = (bf16[512,256]{1,0:T(8,128)(2,1)S(1)}, bf16[512,256]{1,0:T(8,128)(2,1)}, u32[]{:S(2)}) copy-start(bf16[512,256]{1,0:T(8,128)(2,1)} %slopes.11) | copy-start | bytes 786436
  3.6 13.4 %collective-permute-start.2 = (bf16[256,256]{1,0:T(8,128)(2,1)S(1)}, bf16[256,256]{1,0:T(8,128)(2,1)S(1)}, u32[]{:S(2)}, u32[]{:S(2)}) collective-permute-start(bf16[256,256]{1,0:T(8,128)(2,1)S(1)} %get-tuple-element.39), channel_id=1, source_target_pairs={{0,16},{1,17},{2,18},{3,19},{4,20},{5,21},{6,22},{7,23},{8,24},{9,... | collective-permute-start | bytes 393224 | tf_op jit(solution)/shard_map/ppermute | solution.py:149
  7.7 9.3 %collective-permute-start = (bf16[128,256]{1,0:T(8,128)(2,1)S(1)}, bf16[128,256]{1,0:T(8,128)(2,1)S(1)}, u32[]{:S(2)}, u32[]{:S(2)}) collective-permute-start(bf16[128,256]{1,0:T(8,128)(2,1)S(1)} %get-tuple-element.37), channel_id=1, source_target_pairs={{0,1},{1,0},{2,3},{3,2},{4,5},{5,4},{6,7},{7,6},{8,9},{9,8},{10,11... | collective-permute-start | bytes 196616 | tf_op jit(solution)/shard_map/ppermute | solution.py:155
  7.7 9.3 %collective-permute-start.1 = (bf16[128,256]{1,0:T(8,128)(2,1)S(1)}, bf16[128,256]{1,0:T(8,128)(2,1)S(1)}, u32[]{:S(2)}, u32[]{:S(2)}) collective-permute-start(bf16[128,256]{1,0:T(8,128)(2,1)S(1)} %get-tuple-element.38), channel_id=1, source_target_pairs={{0,31},{1,2},{2,1},{3,4},{4,3},{5,6},{6,5},{7,8},{8,7},{9,10},{10,... | collective-permute-start | bytes 196616 | tf_op jit(solution)/shard_map/ppermute | solution.py:154
  11.7 0.7 copy-start.8
  11.8 0.7 copy-start.9
  12.4 1.1 %copy-start.5 = (bf16[24,128,128]{2,1,0:T(8,128)(2,1)S(1)}, bf16[24,128,128]{2,1,0:T(8,128)(2,1)}, u32[]{:S(2)}) copy-start(bf16[24,128,128]{2,1,0:T(8,128)(2,1)} %tiles.1) | copy-start | bytes 2359300
  13.6 0.9 %copy-start.6 = (bf16[512,256]{1,0:T(8,128)(2,1)S(1)}, bf16[512,256]{1,0:T(8,128)(2,1)}, u32[]{:S(2)}) copy-start(bf16[512,256]{1,0:T(8,128)(2,1)} %states.1) | copy-start | bytes 786436
  14.5 2.5 %copy-start.4 = (bf16[256,256]{1,0:T(8,128)(2,1)S(1)}, bf16[256,256]{1,0:T(8,128)(2,1)}, u32[]{:S(2)}) copy-start(bf16[256,256]{1,0:T(8,128)(2,1)} %weight.13) | copy-start | bytes 393220
  17.6 9.7 %collective-permute-start.5 = (bf16[256,256]{1,0:T(8,128)(2,1)S(1)}, bf16[256,256]{1,0:T(8,128)(2,1)S(1)}, u32[]{:S(2)}, u32[]{:S(2)}) collective-permute-start(bf16[256,256]{1,0:T(8,128)(2,1)S(1)} %get-tuple-element.48), channel_id=1, source_target_pairs={{0,16},{1,17},{2,18},{3,19},{4,20},{5,21},{6,22},{7,23},{8,24},{9,... | collective-permute-start | bytes 393224 | tf_op jit(solution)/shard_map/ppermute | solution.py:149
  19.8 1.9 %collective-permute-start.3 = (bf16[128,256]{1,0:T(8,128)(2,1)S(1)}, bf16[128,256]{1,0:T(8,128)(2,1)S(1)}, u32[]{:S(2)}, u32[]{:S(2)}) collective-permute-start(bf16[128,256]{1,0:T(8,128)(2,1)S(1)} %get-tuple-element.46), channel_id=1, source_target_pairs={{0,1},{1,0},{2,3},{3,2},{4,5},{5,4},{6,7},{7,6},{8,9},{9,8},{10,11... | collective-permute-start | bytes 196616 | tf_op jit(solution)/shard_map/ppermute | solution.py:155
  19.9 7.4 %collective-permute-start.4 = (bf16[128,256]{1,0:T(8,128)(2,1)S(1)}, bf16[128,256]{1,0:T(8,128)(2,1)S(1)}, u32[]{:S(2)}, u32[]{:S(2)}) collective-permute-start(bf16[128,256]{1,0:T(8,128)(2,1)S(1)} %get-tuple-element.47), channel_id=1, source_target_pairs={{0,31},{1,2},{2,1},{3,4},{4,3},{5,6},{6,5},{7,8},{8,7},{9,10},{10,... | collective-permute-start | bytes 196616 | tf_op jit(solution)/shard_map/ppermute | solution.py:154
  27.7 8.2 %collective-permute-start.8 = (bf16[256,256]{1,0:T(8,128)(2,1)S(1)}, bf16[256,256]{1,0:T(8,128)(2,1)S(1)}, u32[]{:S(2)}, u32[]{:S(2)}) collective-permute-start(bf16[256,256]{1,0:T(8,128)(2,1)S(1)} %get-tuple-element.56), channel_id=1, source_target_pairs={{0,16},{1,17},{2,18},{3,19},{4,20},{5,21},{6,22},{7,23},{8,24},{9,... | collective-permute-start | bytes 393224 | tf_op jit(solution)/shard_map/ppermute | solution.py:149
  28.6 3.5 %collective-permute-start.6 = (bf16[128,256]{1,0:T(8,128)(2,1)S(1)}, bf16[128,256]{1,0:T(8,128)(2,1)S(1)}, u32[]{:S(2)}, u32[]{:S(2)}) collective-permute-start(bf16[128,256]{1,0:T(8,128)(2,1)S(1)} %get-tuple-element.54), channel_id=1, source_target_pairs={{0,1},{1,0},{2,3},{3,2},{4,5},{5,4},{6,7},{7,6},{8,9},{9,8},{10,11... | collective-permute-start | bytes 196616 | tf_op jit(solution)/shard_map/ppermute | solution.py:155
  28.6 7.4 %collective-permute-start.7 = (bf16[128,256]{1,0:T(8,128)(2,1)S(1)}, bf16[128,256]{1,0:T(8,128)(2,1)S(1)}, u32[]{:S(2)}, u32[]{:S(2)}) collective-permute-start(bf16[128,256]{1,0:T(8,128)(2,1)S(1)} %get-tuple-element.55), channel_id=1, source_target_pairs={{0,31},{1,2},{2,1},{3,4},{4,3},{5,6},{6,5},{7,8},{8,7},{9,10},{10,... | collective-permute-start | bytes 196616 | tf_op jit(solution)/shard_map/ppermute | solution.py:154
  30.3 12.0 %collective-permute-start.12 = (bf16[128,256]{1,0:T(8,128)(2,1)S(1)}, bf16[128,256]{1,0:T(8,128)(2,1)S(1)}, u32[]{:S(2)}, u32[]{:S(2)}) collective-permute-start(bf16[128,256]{1,0:T(8,128)(2,1)S(1)} %get-tuple-element.64), channel_id=1, source_target_pairs={{0,1},{1,0},{2,3},{3,2},{4,5},{5,4},{6,7},{7,6},{8,9},{9,8},{10,11... | collective-permute-start | bytes 196616 | tf_op jit(solution)/shard_map/ppermute | solution.py:155
  30.3 19.4 %collective-permute-start.14 = (bf16[256,256]{1,0:T(8,128)(2,1)S(1)}, bf16[256,256]{1,0:T(8,128)(2,1)S(1)}, u32[]{:S(2)}, u32[]{:S(2)}) collective-permute-start(bf16[256,256]{1,0:T(8,128)(2,1)S(1)} %get-tuple-element.66), channel_id=1, source_target_pairs={{0,16},{1,17},{2,18},{3,19},{4,20},{5,21},{6,22},{7,23},{8,24},{9,... | collective-permute-start | bytes 393224 | tf_op jit(solution)/shard_map/ppermute | solution.py:149
  36.5 15.2 %collective-permute-start.11 = (bf16[256,256]{1,0:T(8,128)(2,1)S(1)}, bf16[256,256]{1,0:T(8,128)(2,1)S(1)}, u32[]{:S(2)}, u32[]{:S(2)}) collective-permute-start(bf16[256,256]{1,0:T(8,128)(2,1)S(1)} %get-tuple-element.61), channel_id=1, source_target_pairs={{0,16},{1,17},{2,18},{3,19},{4,20},{5,21},{6,22},{7,23},{8,24},{9,... | collective-permute-start | bytes 393224 | tf_op jit(solution)/shard_map/ppermute | solution.py:149
  42.3 7.4 %collective-permute-start.13 = (bf16[128,256]{1,0:T(8,128)(2,1)S(1)}, bf16[128,256]{1,0:T(8,128)(2,1)S(1)}, u32[]{:S(2)}, u32[]{:S(2)}) collective-permute-start(bf16[128,256]{1,0:T(8,128)(2,1)S(1)} %get-tuple-element.65), channel_id=1, source_target_pairs={{0,31},{1,2},{2,1},{3,4},{4,3},{5,6},{6,5},{7,8},{8,7},{9,10},{10,... | collective-permute-start | bytes 196616 | tf_op jit(solution)/shard_map/ppermute | solution.py:154
  42.3 9.5 %collective-permute-start.9 = (bf16[128,256]{1,0:T(8,128)(2,1)S(1)}, bf16[128,256]{1,0:T(8,128)(2,1)S(1)}, u32[]{:S(2)}, u32[]{:S(2)}) collective-permute-start(bf16[128,256]{1,0:T(8,128)(2,1)S(1)} %get-tuple-element.59), channel_id=1, source_target_pairs={{0,1},{1,0},{2,3},{3,2},{4,5},{5,4},{6,7},{7,6},{8,9},{9,8},{10,11... | collective-permute-start | bytes 196616 | tf_op jit(solution)/shard_map/ppermute | solution.py:155
  42.3 9.4 %collective-permute-start.10 = (bf16[128,256]{1,0:T(8,128)(2,1)S(1)}, bf16[128,256]{1,0:T(8,128)(2,1)S(1)}, u32[]{:S(2)}, u32[]{:S(2)}) collective-permute-start(bf16[128,256]{1,0:T(8,128)(2,1)S(1)} %get-tuple-element.60), channel_id=1, source_target_pairs={{0,31},{1,2},{2,1},{3,4},{4,3},{5,6},{6,5},{7,8},{8,7},{9,10},{10,... | collective-permute-start | bytes 196616 | tf_op jit(solution)/shard_map/ppermute | solution.py:154
  53.1 2.4 %collective-permute-start.15 = (f32[256,256]{1,0:T(8,128)S(1)}, f32[256,256]{1,0:T(8,128)S(1)}, u32[]{:S(2)}, u32[]{:S(2)}) collective-permute-start(f32[256,256]{1,0:T(8,128)S(1)} %get-tuple-element.71), channel_id=1, source_target_pairs={{0,1},{2,3},{4,5},{6,7},{8,9},{10,11},{12,13},{14,15},{16,17},{18,... | collective-permute-start | bytes 786440 | tf_op jit(solution)/shard_map/ppermute | solution.py:163
  55.5 0.7 collective-permute-start.16
  56.3 0.7 collective-permute-start.17
  57.0 0.7 collective-permute-start.18
  57.7 0.7 collective-permute-start.19
  58.5 24.8 %collective-permute-start.20 = (f32[256,256]{1,0:T(8,128)S(1)}, f32[256,256]{1,0:T(8,128)S(1)}, u32[]{:S(2)}, u32[]{:S(2)}) collective-permute-start(f32[256,256]{1,0:T(8,128)S(1)} %convert_add_fusion), channel_id=1, source_target_pairs={{1,0},{3,2},{5,4},{7,6},{9,8},{11,10},{13,12},{15,14},{17,16},{19,... | collective-permute-start | bytes 786440 | tf_op jit(solution)/shard_map/ppermute | solution.py:171

commit v2 on v1

v2 whole, which is shorter than its diff:
```python
import functools

import jax
import jax.numpy as jnp
from jax import lax
from jax.experimental import pallas as pl
from jax.experimental.pallas import tpu as pltpu
from jax.sharding import PartitionSpec as P


ITERS = 4
REACH = 16
LISTS = 4
BF = jnp.bfloat16
F32 = jnp.float32
VMEM_BYTES = 8 * 1024 * 1024


def call(body, outs, ins, scratch=()):
    spaces = {"v": pltpu.VMEM, "s": pltpu.SMEM, "h": pltpu.HBM}
    return pl.pallas_call(
        body,
        out_shape=tuple(jax.ShapeDtypeStruct(shape, dtype) for shape, dtype in outs),
        in_specs=[pl.BlockSpec(memory_space=spaces[kind]) for kind in ins],
        out_specs=tuple(pl.BlockSpec(memory_space=pltpu.VMEM) for _ in outs),
        scratch_shapes=list(scratch),
        compiler_params=pltpu.CompilerParams(vmem_limit_bytes=VMEM_BYTES),
    )


def in_hbm(*arrays):
    return [pltpu.with_memory_space_constraint(a, pltpu.HBM) for a in arrays]


def mm(a, b):
    return jnp.dot(a, b, preferred_element_type=F32)


def mm_rhs_t(a, b):
    return lax.dot_general(a, b, (((1,), (1,)), ((), ())), preferred_element_type=F32)


def mm_lhs_t(a, b):
    return lax.dot_general(a, b, (((0,), (0,)), ((), ())), preferred_element_type=F32)


def parity():
    return lax.rem(lax.axis_index("dom"), 2)


def side():
    index = lax.axis_index("dom")
    bits = (lax.axis_size("dom") - 1).bit_length()
    result = index & 1
    for bit in range(1, bits):
        result = result ^ ((index >> bit) & 1)
    return result


def first_body(
    lists_in, grad_in, slopes_in, tiles_in, states_in, weight_in,
    near, far, wide, scaled, pick, grad, slopes, tiles, states, weight, lists, sems,
):
    pairs = (
        (lists_in, lists), (grad_in, grad), (slopes_in, slopes),
        (tiles_in, tiles), (states_in, states), (weight_in, weight),
    )
    copies = [pltpu.make_async_copy(source, held, sems.at[n]) for n, (source, held) in enumerate(pairs)]
    for copy in copies:
        copy.start()
    size = lists.shape[1]
    rows = grad.shape[0]
    odd = parity() == 1
    copies[0].wait()
    order = (
        jnp.where(odd, lists[1:2, :], lists[0:1, :]),
        jnp.where(odd, lists[0:1, :], lists[1:2, :]),
        lists[2:3, :],
        lists[3:4, :],
    )
    column = lax.broadcasted_iota(jnp.int32, (size, rows), 1)
    for n in range(LISTS):
        wanted = jnp.broadcast_to(order[n], (size, size)).astype(F32).T.astype(jnp.int32)
        wanted = jnp.concatenate([wanted] * (rows // size), axis=1)
        pick[n * size : (n + 1) * size, :] = (wanted == column).astype(F32).astype(BF)
    copies[1].wait()
    copies[2].wait()
    value = (slopes[...].astype(F32) * grad[...].astype(F32)).astype(BF)
    scaled[...] = value
    sent = mm(pick[...], value).astype(BF)
    near[...] = sent[:size]
    far[...] = sent[size : 2 * size]
    wide[...] = sent[2 * size :]
    for copy in copies[3:]:
        copy.wait()


def setup_body(
    dst_in, src_in, count, tiles, pick, grad, slopes, scaled, states,
    own, edge, pick_own, pick_edge, pick_grad, pick_slopes, local, pick_local,
    back_own, back_near, back_far, back_wide, total, dst, src, sems,
):
    pairs = ((dst_in, dst), (src_in, src))
    copies = [pltpu.make_async_copy(source, held, sems.at[n]) for n, (source, held) in enumerate(pairs)]
    for copy in copies:
        copy.start()
    size = tiles.shape[1]
    blocks = total.shape[0]
    half = blocks // 2
    even = parity() == 0
    total[...] = jnp.zeros_like(total)
    chosen = pick[...]
    pick_grad[...] = mm(chosen, grad[...]).astype(BF)
    pick_slopes[...] = mm(chosen, slopes[...]).astype(BF)
    for copy in copies:
        copy.wait()

    def add(slot, carry):
        source = src[slot]
        swapped = even & ((source == half) | (source == half + 1))
        source = jnp.where(swapped, 2 * half + 1 - source, source)
        at = pl.ds(pl.multiple_of(dst[slot] * size, size), size)
        total[source, at, :] = total[source, at, :] + tiles[slot].astype(F32)
        return carry

    lax.fori_loop(0, count[0], add, 0)
    for b in range(half):
        at = slice(b * size, (b + 1) * size)
        own[:, at] = total[b].astype(BF)
        edge[:, at] = total[half + b].astype(BF)
    pick_own[...] = mm(chosen, own[...]).astype(BF)
    pick_edge[...] = mm(chosen, edge[...]).astype(BF)
    local[...] = mm(own[...], scaled[...])
    pick_local[...] = mm(pick_own[...], scaled[...])
    back_own[...] = mm_lhs_t(own[...], states[...])
    back = mm_lhs_t(edge[...], states[...]).astype(BF)
    back_near[...] = back[:size]
    back_far[...] = back[size : 2 * size]
    back_wide[...] = back[2 * size :]


def arrived(near, far, wide):
    size = wide.shape[0] // 2
    return jnp.concatenate([near[:size, :], far[:size, :], wide[...]], axis=0)


def send_body(
    near, far, wide, pick_local, pick_edge, pick_grad, pick_slopes, weight, *rest
):
    near_out, far_out, wide_out = rest[-3:]
    size = wide.shape[0] // 2
    came = arrived(near, far, wide)
    mixed = (pick_local[...] + mm(pick_edge[...], came)).astype(BF)
    adjoint = pick_grad[...].astype(F32) + mm_rhs_t(mixed, weight[...])
    sent = (pick_slopes[...].astype(F32) * adjoint).astype(BF)
    near_out[:size, :] = sent[:size]
    far_out[:size, :] = sent[size : 2 * size]
    wide_out[...] = sent[2 * size :]
    if len(rest) > 3:
        near_out[size:, :] = rest[0][...]
        far_out[size:, :] = rest[1][...]


def newest(near, far, wide, local, edge, grad, weight):
    mixed = (local[...] + mm(edge[...], arrived(near, far, wide))).astype(BF)
    return grad[...].astype(F32) + mm_rhs_t(mixed, weight[...])


def own_body(near, far, wide, local, edge, grad, slopes, weight, own, pick_own, local_out, pick_local_out):
    scaled = (slopes[...].astype(F32) * newest(near, far, wide, local, edge, grad, weight)).astype(BF)
    local_out[...] = mm(own[...], scaled)
    pick_local_out[...] = mm(pick_own[...], scaled)


def back_body(near, far, wide, back_own, pick, high, low):
    size = wide.shape[0] // 2
    came = jnp.concatenate([near[size:, :], far[size:, :], wide[...]], axis=0)
    value = (back_own[...] + mm_lhs_t(pick[...], came)).T
    top = value.astype(BF)
    high[...] = top
    low[...] = (value - top.astype(F32)).astype(BF)


def last_body(factor, near, far, wide, local, edge, grad, slopes, weight, high, low, kept, given):
    scaled = (slopes[...].astype(F32) * newest(near, far, wide, local, edge, grad, weight)).astype(BF)
    rows = kept.shape[0]
    at = side()
    for half, out in ((at, kept), (1 - at, given)):
        lines = pl.ds(pl.multiple_of(half * rows, rows), rows)
        out[...] = (mm(high[lines, :], scaled) + mm(low[lines, :], scaled)) * factor


def adjoint_body(near, far, wide, local, edge, grad, weight, out):
    out[...] = newest(near, far, wide, local, edge, grad, weight)


def join_body(total, other, out):
    rows = total.shape[0]
    at = side()
    out[pl.ds(pl.multiple_of(at * rows, rows), rows), :] = total[...]
    out[pl.ds(pl.multiple_of((1 - at) * rows, rows), rows), :] = other[...]


def swap_wide(wide, forward=True):
    count = lax.axis_size("dom")
    ahead = [(p, (p + REACH) % count) for p in range(count)]
    behind = [(p, (p - REACH) % count) for p in range(count)]
    if not forward:
        ahead, behind = behind, ahead
    if ahead == behind:
        return lax.ppermute(wide, "dom", ahead)
    size = wide.shape[0] // 2
    return jnp.concatenate(
        [lax.ppermute(wide[:size], "dom", ahead), lax.ppermute(wide[size:], "dom", behind)], axis=0
    )


def exchange(near, far, wide):
    count = lax.axis_size("dom")
    wide = swap_wide(wide)
    far = lax.ppermute(far, "dom", [(p, (p + 1 if p % 2 else p - 1) % count) for p in range(count)])
    near = lax.ppermute(near, "dom", [(p, p ^ 1) for p in range(count)])
    return near, far, wide


def summed(kept, given):
    count = lax.axis_size("dom")
    rows, width = kept.shape
    beside = [(p, p ^ 1) for p in range(count)]
    total = kept + lax.ppermute(given, "dom", beside)
    step = 2
    while step < count:
        mine = total.astype(BF)
        theirs = lax.ppermute(mine, "dom", [(p, p ^ step ^ 1) for p in range(count)])
        total = mine.astype(F32) + theirs.astype(F32)
        step *= 2
    other = lax.ppermute(total, "dom", beside)
    return call(join_body, [((2 * rows, width), F32)], "vv")(total, other)[0]


def per_device(grad_out, states, slopes, weight, tiles, tile_dst, tile_src, tile_count, send_rows):
    rows, width = grad_out.shape
    slots, size, _ = tiles.shape
    cut = LISTS * size
    blocks = rows // size + LISTS
    field = (rows, width)
    message = [((size, width), BF), ((size, width), BF), ((2 * size, width), BF)]
    longer = [((2 * size, width), BF)] * 3

    near, far, wide, scaled, pick, grad_out, slopes, tiles, states, weight = call(
        first_body,
        message + [
            (field, BF), ((cut, rows), BF), (field, BF), (field, BF), (tiles.shape, BF), (field, BF),
            (weight.shape, BF),
        ],
        "hhhhhh",
        [pltpu.VMEM(send_rows.shape, jnp.int32), pltpu.SemaphoreType.DMA((6,))],
    )(*in_hbm(send_rows, grad_out, slopes, tiles, states, weight))
    came = exchange(near, far, wide)
    (
        own, edge, pick_own, pick_edge, pick_grad, pick_slopes, local, pick_local, back_own,
        back_near, back_far, back_wide,
    ) = call(
        setup_body,
        [
            ((rows, rows), BF), ((rows, cut), BF), ((cut, rows), BF), ((cut, cut), BF),
            ((cut, width), BF), ((cut, width), BF), (field, F32), ((cut, width), F32),
            (field, F32),
        ] + message,
        "hhsvvvvvv",
        [
            pltpu.VMEM((blocks, rows, size), F32), pltpu.SMEM((slots,), jnp.int32),
            pltpu.SMEM((slots,), jnp.int32), pltpu.SemaphoreType.DMA((2,)),
        ],
    )(*in_hbm(tile_dst, tile_src), tile_count, tiles, pick, grad_out, slopes, scaled, states)

    for step in range(ITERS - 1):
        extra = (back_near, back_far) if step == 0 else ()
        operands = (*came, pick_local, pick_edge, pick_grad, pick_slopes, weight, *extra)
        sent = call(send_body, longer if extra else message, "v" * len(operands))(*operands)
        following = exchange(*sent)
        if step == 0:
            back_wide = swap_wide(back_wide, False)
        local, pick_local = call(own_body, [(field, F32), ((cut, width), F32)], "v" * 10)(
            *came, local, edge, grad_out, slopes, weight, own, pick_own
        )
        came = following
        if step == 0:
            back_came = (came[0], came[1], back_wide)
    high, low = call(back_body, [((width, rows), BF), ((width, rows), BF)], "vvvvv")(*back_came, back_own, pick)
    factor = 1.0 / float(lax.axis_size("dom") * rows) ** 0.5
    half = ((width // 2, width), F32)
    kept, given = call(functools.partial(last_body, factor), [half, half], "v" * 10)(
        *came, local, edge, grad_out, slopes, weight, high, low
    )
    (adjoint,) = call(adjoint_body, [(field, F32)], "v" * 7)(*came, local, edge, grad_out, weight)
    return adjoint, summed(kept, given)


def solution(mesh):
    in_specs = (
        P("dom", None),
        P("dom", None),
        P("dom", None),
        P(),
        P("dom", None, None),
        P("dom"),
        P("dom"),
        P("dom"),
        P("dom", None),
    )
    out_specs = (P("dom", None), P())
    return jax.shard_map(per_device, mesh=mesh, in_specs=in_specs, out_specs=out_specs, check_vma=False)
```

time: 84.4 us -> 72.4 us (0.86)
  starting transfers between devices: 30.7 us -> 22.6 us
  local copies, waits for them, and re-layouts: 5.3 us -> 0 us
  Pallas kernels: 9.45 us -> 11.7 us
    ppermute x16 -> x15, starting transfers between devices: 19.3 us -> 10.3 us  [the longest x5 9.36 us: swap_wide(): return lax.ppermute(wide, 'dom', ahead)]
    unnamed x20 -> x0, local copies, waits for them, and re-layouts: 5.3 us -> none
    pallas_call x8 -> x10, Pallas kernels: 6.52 us -> 9.01 us  [the longest x3 3.31 us: per_device(): call(own_body, [(field, F32), ((cut, width), F32)], 'v' * 10)]
    ppermute x5 -> x4, starting transfers between devices: 11.4 us -> 12.3 us  [exchange(): lax.ppermute(far, 'dom', [(p, (p + 1 if p % 2 else p - 1) % count) for p...]
    ppermute x5 -> x4, waiting for transfers between devices: 11.4 us -> 11.6 us  [exchange(): lax.ppermute(far, 'dom', [(p, (p + 1 if p % 2 else p - 1) % count) for p...]
    ppermute x16 -> x15, waiting for transfers between devices: 24.7 us -> 24.8 us  [the longest x4 17.8 us: summed(): lax.ppermute(mine, 'dom', [(p, p ^ step ^ 1) for p in range(count)])]
  transfers between devices with their start and end apart: 21 -> 19, of which waited for: 5 -> 11; matrix products, arithmetic and copies ran while one was open for 0% -> 0% of each run, Pallas kernels for 8% -> 11%
where the time goes in v2:
time: 72.4 us; the launch traced here: 72.2 us
  waiting for transfers between devices  36.3 us (50%)
  starting transfers between devices  22.6 us (31%)
  Pallas kernels  11.7 us (16%)
  between operations  1.43 us (2%)
    ppermute x4, waiting for transfers between devices, summed(): lax.ppermute(mine, 'dom', [(p, p ^ step ^ 1) for p in range(count)])  17.8 us
    ppermute x4, starting transfers between devices, exchange(): lax.ppermute(far, 'dom', [(p, (p + 1 if p % 2 else p - 1) % count) for p...  12.3 us
    ppermute x4, waiting for transfers between devices, exchange(): lax.ppermute(far, 'dom', [(p, (p + 1 if p % 2 else p - 1) % count) for p...  11.6 us
    ppermute x5, starting transfers between devices, swap_wide(): return lax.ppermute(wide, 'dom', ahead)  9.36 us
    ppermute x5, waiting for transfers between devices, swap_wide(): return lax.ppermute(wide, 'dom', ahead)  5.64 us
    pallas_call x3, Pallas kernels, per_device(): call(own_body, [(field, F32), ((cut, width), F32)], 'v' * 10)  3.31 us
    pallas_call x1, Pallas kernels, per_device(): call(setup_body, [((rows, rows), BF), ((rows, cut), BF), ((cut, rows), BF...  2.26 us
    pallas_call x3, Pallas kernels, per_device(): call(send_body, longer if extra else message, 'v' * len(operands))  1.49 us
  transfers between devices with their start and end apart: 19, of which 11 were waited for; matrix products, arithmetic and copies ran while one was open for 0% of the time, Pallas kernels for 11%

profile of v2, /device:TPU:0, one launch (start us, length us, event | category | flops | bytes accessed | tf_op | source)
XLA Modules:
  0.0 72.2 jit_solution(9636788451137638344)
XLA Ops:
  0.6 1.4 %shard_map.104 = (bf16[128,256]{1,0:T(8,128)(2,1)S(1)}, bf16[128,256]{1,0:T(8,128)(2,1)S(1)}, bf16[256,256]{1,0:T(8,128)(2,1)S(1)}, bf16[512,256]{1,0:T(8,128)(2...) custom-call(s32[4,128]{1,0:T(4,128)} %lists_in.1, ...), custom_call_target="tpu_custom_call" | custom-call | tf_op jit(solution)/shard_map/pallas_call | solution.py:250
  2.1 4.1 %collective-permute-start.2 = (bf16[256,256]{1,0:T(8,128)(2,1)S(1)}, bf16[256,256]{1,0:T(8,128)(2,1)S(1)}, u32[]{:S(2)}, u32[]{:S(2)}) collective-permute-start(bf16[256,256]{1,0:T(8,128)(2,1)S(1)} %get-tuple-element.44), channel_id=1, source_target_pairs={{0,16},{1,17},{2,18},{3,19},{4,20},{5,21},{6,22},{7,23},{8,24},{9,... | collective-permute-start | bytes 393224 | tf_op jit(solution)/shard_map/ppermute | solution.py:211
  6.2 0.0 collective-permute-start
  6.2 3.3 %collective-permute-start.1 = (bf16[128,256]{1,0:T(8,128)(2,1)S(1)}, bf16[128,256]{1,0:T(8,128)(2,1)S(1)}, u32[]{:S(2)}, u32[]{:S(2)}) collective-permute-start(bf16[128,256]{1,0:T(8,128)(2,1)S(1)} %get-tuple-element.43), channel_id=1, source_target_pairs={{0,31},{1,2},{2,1},{3,4},{4,3},{5,6},{6,5},{7,8},{8,7},{9,10},{10,... | collective-permute-start | bytes 196616 | tf_op jit(solution)/shard_map/ppermute | solution.py:221
  10.2 2.3 %shard_map.105 = (bf16[512,512]{1,0:T(8,128)(2,1)S(1)}, bf16[512,512]{1,0:T(8,128)(2,1)S(1)}, bf16[512,512]{1,0:T(8,128)(2,1)S(1)}, bf16[512,512]{1,0:T(8,128)(2...) custom-call(s32[24]{0:T(128)} %dst_in.1, ...), custom_call_target="tpu_custom_call" | custom-call | tf_op jit(solution)/shard_map/pallas_call | solution.py:263
  12.5 0.0 collective-permute-done.near
  12.5 1.0 %collective-permute-done.1.far = bf16[128,256]{1,0:T(8,128)(2,1)S(1)} collective-permute-done((bf16[128,256]{1,0:T(8,128)(2,1)S(1)}, bf16[128,256]{1,0:T(8,128)(2,1)S(1)}, u32[]{:S(2)}, u32[]{:S(2)}) %collective-permute-start.1) | collective-permute-done | bytes 65568 | tf_op jit(solution)/shard_map/ppermute | solution.py:221
  13.5 0.0 collective-permute-done.2.wide
  13.5 0.5 shard_map.106
  14.0 0.1 collective-permute-start.3
  14.1 4.6 %collective-permute-start.4 = (bf16[256,256]{1,0:T(8,128)(2,1)S(1)}, bf16[256,256]{1,0:T(8,128)(2,1)S(1)}, u32[]{:S(2)}, u32[]{:S(2)}) collective-permute-start(bf16[256,256]{1,0:T(8,128)(2,1)S(1)} %get-tuple-element.59), channel_id=1, source_target_pairs={{0,31},{1,2},{2,1},{3,4},{4,3},{5,6},{6,5},{7,8},{8,7},{9,10},{10,... | collective-permute-start | bytes 393224 | tf_op jit(solution)/shard_map/ppermute | solution.py:221
  18.7 0.0 collective-permute-start.5
  18.7 0.8 %shard_map.107 = (f32[512,256]{1,0:T(8,128)S(1)}, f32[512,256]{1,0:T(8,128)S(1)}) custom-call(bf16[128,256]{1,0:T(8,128)(2,1)S(1)} %collective-permute-done.near, bf16[128,256]{1,0:T(8,128)(2,1)S(1)} %collective-permute-done.1.far, bf16[256,256]{1,0:T(8,128)(2,1)S(1)} %collective-permute-done.2.wide, f32[512,256]{1,0:T(8,128)S(1)} %get-tuple-element.61.local, ...), custom_call_target="tpu_custom_call" | custom-call | tf_op jit(solution)/shard_map/pallas_call | solution.py:284
  19.6 0.0 collective-permute-done.3.near
  19.6 4.0 %collective-permute-done.4.far = bf16[256,256]{1,0:T(8,128)(2,1)S(1)} collective-permute-done((bf16[256,256]{1,0:T(8,128)(2,1)S(1)}, bf16[256,256]{1,0:T(8,128)(2,1)S(1)}, u32[]{:S(2)}, u32[]{:S(2)}) %collective-permute-start.4) | collective-permute-done | bytes 131104 | tf_op jit(solution)/shard_map/ppermute | solution.py:221
  23.6 2.8 %collective-permute-done.5.wide = bf16[256,256]{1,0:T(8,128)(2,1)S(1)} collective-permute-done((bf16[256,256]{1,0:T(8,128)(2,1)S(1)}, bf16[256,256]{1,0:T(8,128)(2,1)S(1)}, u32[]{:S(2)}, u32[]{:S(2)}) %collective-permute-start.5) | collective-permute-done | bytes 131104 | tf_op jit(solution)/shard_map/ppermute | solution.py:211
  26.4 0.5 shard_map.108
  26.9 0.8 %collective-permute-start.8 = (bf16[256,256]{1,0:T(8,128)(2,1)S(1)}, bf16[256,256]{1,0:T(8,128)(2,1)S(1)}, u32[]{:S(2)}, u32[]{:S(2)}) collective-permute-start(bf16[256,256]{1,0:T(8,128)(2,1)S(1)} %get-tuple-element.68), channel_id=1, source_target_pairs={{0,16},{1,17},{2,18},{3,19},{4,20},{5,21},{6,22},{7,23},{8,24},{9,... | collective-permute-start | bytes 393224 | tf_op jit(solution)/shard_map/ppermute | solution.py:211
  27.7 0.0 collective-permute-start.6
  27.7 1.9 %collective-permute-start.7 = (bf16[128,256]{1,0:T(8,128)(2,1)S(1)}, bf16[128,256]{1,0:T(8,128)(2,1)S(1)}, u32[]{:S(2)}, u32[]{:S(2)}) collective-permute-start(bf16[128,256]{1,0:T(8,128)(2,1)S(1)} %get-tuple-element.67), channel_id=1, source_target_pairs={{0,31},{1,2},{2,1},{3,4},{4,3},{5,6},{6,5},{7,8},{8,7},{9,10},{10,... | collective-permute-start | bytes 196616 | tf_op jit(solution)/shard_map/ppermute | solution.py:221
  29.6 1.6 %collective-permute-start.12 = (bf16[256,256]{1,0:T(8,128)(2,1)S(1)}, bf16[256,256]{1,0:T(8,128)(2,1)S(1)}, u32[]{:S(2)}, u32[]{:S(2)}) collective-permute-start(bf16[256,256]{1,0:T(8,128)(2,1)S(1)} %get-tuple-element.76), channel_id=1, source_target_pairs={{0,16},{1,17},{2,18},{3,19},{4,20},{5,21},{6,22},{7,23},{8,24},{9,... | collective-permute-start | bytes 393224 | tf_op jit(solution)/shard_map/ppermute | solution.py:211
  31.2 0.8 %shard_map.109 = (f32[512,256]{1,0:T(8,128)S(1)}, f32[512,256]{1,0:T(8,128)S(1)}) custom-call(bf16[256,256]{1,0:T(8,128)(2,1)S(1)} %collective-permute-done.3.near, bf16[256,256]{1,0:T(8,128)(2,1)S(1)} %collective-permute-done.4.far, bf16[256,256]{1,0:T(8,128)(2,1)S(1)} %collective-permute-done.5.wide, f32[512,256]{1,0:T(8,128)S(1)} %get-tuple-element.69.local, ...), custom_call_target="tpu_custom_call" | custom-call | tf_op jit(solution)/shard_map/pallas_call | solution.py:284
  32.0 0.0 collective-permute-done.6.near
  32.1 3.8 %collective-permute-done.7.far = bf16[128,256]{1,0:T(8,128)(2,1)S(1)} collective-permute-done((bf16[128,256]{1,0:T(8,128)(2,1)S(1)}, bf16[128,256]{1,0:T(8,128)(2,1)S(1)}, u32[]{:S(2)}, u32[]{:S(2)}) %collective-permute-start.7) | collective-permute-done | bytes 65568 | tf_op jit(solution)/shard_map/ppermute | solution.py:221
  35.8 2.8 %collective-permute-done.8.wide = bf16[256,256]{1,0:T(8,128)(2,1)S(1)} collective-permute-done((bf16[256,256]{1,0:T(8,128)(2,1)S(1)}, bf16[256,256]{1,0:T(8,128)(2,1)S(1)}, u32[]{:S(2)}, u32[]{:S(2)}) %collective-permute-start.8) | collective-permute-done | bytes 131104 | tf_op jit(solution)/shard_map/ppermute | solution.py:211
  38.6 0.5 shard_map.110
  39.1 2.9 %collective-permute-start.11 = (bf16[256,256]{1,0:T(8,128)(2,1)S(1)}, bf16[256,256]{1,0:T(8,128)(2,1)S(1)}, u32[]{:S(2)}, u32[]{:S(2)}) collective-permute-start(bf16[256,256]{1,0:T(8,128)(2,1)S(1)} %get-tuple-element.73), channel_id=1, source_target_pairs={{0,16},{1,17},{2,18},{3,19},{4,20},{5,21},{6,22},{7,23},{8,24},{9,... | collective-permute-start | bytes 393224 | tf_op jit(solution)/shard_map/ppermute | solution.py:211
  42.0 0.0 collective-permute-start.9
  42.0 2.5 %collective-permute-start.10 = (bf16[128,256]{1,0:T(8,128)(2,1)S(1)}, bf16[128,256]{1,0:T(8,128)(2,1)S(1)}, u32[]{:S(2)}, u32[]{:S(2)}) collective-permute-start(bf16[128,256]{1,0:T(8,128)(2,1)S(1)} %get-tuple-element.72), channel_id=1, source_target_pairs={{0,31},{1,2},{2,1},{3,4},{4,3},{5,6},{6,5},{7,8},{8,7},{9,10},{10,... | collective-permute-start | bytes 196616 | tf_op jit(solution)/shard_map/ppermute | solution.py:221
  44.5 0.0 collective-permute-done.12.wide
  44.5 0.4 shard_map.113
  44.9 1.6 %shard_map.111 = (f32[512,256]{1,0:T(8,128)S(1)}, f32[512,256]{1,0:T(8,128)}) custom-call(bf16[128,256]{1,0:T(8,128)(2,1)S(1)} %collective-permute-done.6.near, bf16[128,256]{1,0:T(8,128)(2,1)S(1)} %collective-permute-done.7.far, bf16[256,256]{1,0:T(8,128)(2,1)S(1)} %collective-permute-done.8.wide, f32[512,256]{1,0:T(8,128)S(1)} %get-tuple-element.74.local, ...), custom_call_target="tpu_custom_call" | custom-call | tf_op jit(solution)/shard_map/pallas_call | solution.py:284
  46.5 0.0 collective-permute-done.9.near
  46.5 2.7 %collective-permute-done.10.far = bf16[128,256]{1,0:T(8,128)(2,1)S(1)} collective-permute-done((bf16[128,256]{1,0:T(8,128)(2,1)S(1)}, bf16[128,256]{1,0:T(8,128)(2,1)S(1)}, u32[]{:S(2)}, u32[]{:S(2)}) %collective-permute-start.10) | collective-permute-done | bytes 65568 | tf_op jit(solution)/shard_map/ppermute | solution.py:221
  49.3 0.8 %shard_map.114 = (f32[128,256]{1,0:T(8,128)S(1)}, f32[128,256]{1,0:T(8,128)S(1)}) custom-call(bf16[128,256]{1,0:T(8,128)(2,1)S(1)} %collective-permute-done.9.near, bf16[128,256]{1,0:T(8,128)(2,1)S(1)} %collective-permute-done.10.far, bf16[256,256]{1,0:T(8,128)(2,1)S(1)} %collective-permute-done.11.wide, f32[512,256]{1,0:T(8,128)S(1)} %get-tuple-element.75.local, ...), custom_call_target="tpu_custom_call" | custom-call | tf_op jit(solution)/shard_map/pallas_call | solution.py:293
  50.0 0.1 collective-permute-start.13
  50.1 1.3 %collective-permute-done.13 = f32[128,256]{1,0:T(8,128)S(1)} collective-permute-done((f32[128,256]{1,0:T(8,128)S(1)}, f32[128,256]{1,0:T(8,128)S(1)}, u32[]{:S(2)}, u32[]{:S(2)}) %collective-permute-start.13) | collective-permute-done | bytes 131104 | tf_op jit(solution)/shard_map/ppermute | solution.py:230
  51.5 0.1 collective-permute-start.14
  51.5 4.0 %collective-permute-done.14 = bf16[128,256]{1,0:T(8,128)(2,1)S(1)} collective-permute-done((bf16[128,256]{1,0:T(8,128)(2,1)S(1)}, bf16[128,256]{1,0:T(8,128)(2,1)S(1)}, u32[]{:S(2)}, u32[]{:S(2)}) %collective-permute-start.14) | collective-permute-done | bytes 65568 | tf_op jit(solution)/shard_map/ppermute | solution.py:234
  55.6 0.1 collective-permute-start.15
  55.7 4.0 %collective-permute-done.15 = bf16[128,256]{1,0:T(8,128)(2,1)S(1)} collective-permute-done((bf16[128,256]{1,0:T(8,128)(2,1)S(1)}, bf16[128,256]{1,0:T(8,128)(2,1)S(1)}, u32[]{:S(2)}, u32[]{:S(2)}) %collective-permute-start.15) | collective-permute-done | bytes 65568 | tf_op jit(solution)/shard_map/ppermute | solution.py:234
  59.8 0.1 collective-permute-start.16
  59.8 4.0 %collective-permute-done.16 = bf16[128,256]{1,0:T(8,128)(2,1)S(1)} collective-permute-done((bf16[128,256]{1,0:T(8,128)(2,1)S(1)}, bf16[128,256]{1,0:T(8,128)(2,1)S(1)}, u32[]{:S(2)}, u32[]{:S(2)}) %collective-permute-start.16) | collective-permute-done | bytes 65568 | tf_op jit(solution)/shard_map/ppermute | solution.py:234
  63.9 0.4 collective-permute-start.17
  64.3 5.7 %collective-permute-done.17 = bf16[128,256]{1,0:T(8,128)(2,1)S(1)} collective-permute-done((bf16[128,256]{1,0:T(8,128)(2,1)S(1)}, bf16[128,256]{1,0:T(8,128)(2,1)S(1)}, u32[]{:S(2)}, u32[]{:S(2)}) %collective-permute-start.17) | collective-permute-done | bytes 65568 | tf_op jit(solution)/shard_map/ppermute | solution.py:234
  70.0 0.2 collective-permute-start.18
  70.2 1.3 %shard_map.112 = f32[512,256]{1,0:T(8,128)} custom-call(bf16[128,256]{1,0:T(8,128)(2,1)S(1)} %collective-permute-done.9.near, bf16[128,256]{1,0:T(8,128)(2,1)S(1)} %collective-permute-done.10.far, bf16[256,256]{1,0:T(8,128)(2,1)S(1)} %collective-permute-done.11.wide, f32[512,256]{1,0:T(8,128)S(1)} %get-tuple-element.75.local, ...), custom_call_target="tpu_custom_call" | custom-call | tf_op jit(solution)/shard_map/pallas_call | solution.py:296
  71.4 0.7 %shard_map.115 = f32[256,256]{1,0:T(8,128)} custom-call(f32[128,256]{1,0:T(8,128)S(1)} %convert_add_fusion.total, f32[128,256]{1,0:T(8,128)S(1)} %collective-permute-done.18.other), custom_call_target="tpu_custom_call" | custom-call | tf_op jit(solution)/shard_map/pallas_call | solution.py:238
  (7 shorter events, 0.1 us)
Async XLA Ops:
  2.1 11.4 %collective-permute-start.2 = (bf16[256,256]{1,0:T(8,128)(2,1)S(1)}, bf16[256,256]{1,0:T(8,128)(2,1)S(1)}, u32[]{:S(2)}, u32[]{:S(2)}) collective-permute-start(bf16[256,256]{1,0:T(8,128)(2,1)S(1)} %get-tuple-element.44), channel_id=1, source_target_pairs={{0,16},{1,17},{2,18},{3,19},{4,20},{5,21},{6,22},{7,23},{8,24},{9,... | collective-permute-start | bytes 393224 | tf_op jit(solution)/shard_map/ppermute | solution.py:211
  6.2 6.3 %collective-permute-start = (bf16[128,256]{1,0:T(8,128)(2,1)S(1)}, bf16[128,256]{1,0:T(8,128)(2,1)S(1)}, u32[]{:S(2)}, u32[]{:S(2)}) collective-permute-start(bf16[128,256]{1,0:T(8,128)(2,1)S(1)} %get-tuple-element.42), channel_id=1, source_target_pairs={{0,1},{1,0},{2,3},{3,2},{4,5},{5,4},{6,7},{7,6},{8,9},{9,8},{10,11... | collective-permute-start | bytes 196616 | tf_op jit(solution)/shard_map/ppermute | solution.py:222
  6.2 7.3 %collective-permute-start.1 = (bf16[128,256]{1,0:T(8,128)(2,1)S(1)}, bf16[128,256]{1,0:T(8,128)(2,1)S(1)}, u32[]{:S(2)}, u32[]{:S(2)}) collective-permute-start(bf16[128,256]{1,0:T(8,128)(2,1)S(1)} %get-tuple-element.43), channel_id=1, source_target_pairs={{0,31},{1,2},{2,1},{3,4},{4,3},{5,6},{6,5},{7,8},{8,7},{9,10},{10,... | collective-permute-start | bytes 196616 | tf_op jit(solution)/shard_map/ppermute | solution.py:221
  14.0 5.5 %collective-permute-start.3 = (bf16[256,256]{1,0:T(8,128)(2,1)S(1)}, bf16[256,256]{1,0:T(8,128)(2,1)S(1)}, u32[]{:S(2)}, u32[]{:S(2)}) collective-permute-start(bf16[256,256]{1,0:T(8,128)(2,1)S(1)} %get-tuple-element.58), channel_id=1, source_target_pairs={{0,1},{1,0},{2,3},{3,2},{4,5},{5,4},{6,7},{7,6},{8,9},{9,8},{10,11... | collective-permute-start | bytes 393224 | tf_op jit(solution)/shard_map/ppermute | solution.py:222
  14.1 9.5 %collective-permute-start.4 = (bf16[256,256]{1,0:T(8,128)(2,1)S(1)}, bf16[256,256]{1,0:T(8,128)(2,1)S(1)}, u32[]{:S(2)}, u32[]{:S(2)}) collective-permute-start(bf16[256,256]{1,0:T(8,128)(2,1)S(1)} %get-tuple-element.59), channel_id=1, source_target_pairs={{0,31},{1,2},{2,1},{3,4},{4,3},{5,6},{6,5},{7,8},{8,7},{9,10},{10,... | collective-permute-start | bytes 393224 | tf_op jit(solution)/shard_map/ppermute | solution.py:221
  18.7 7.7 %collective-permute-start.5 = (bf16[256,256]{1,0:T(8,128)(2,1)S(1)}, bf16[256,256]{1,0:T(8,128)(2,1)S(1)}, u32[]{:S(2)}, u32[]{:S(2)}) collective-permute-start(bf16[256,256]{1,0:T(8,128)(2,1)S(1)} %get-tuple-element.60), channel_id=1, source_target_pairs={{0,16},{1,17},{2,18},{3,19},{4,20},{5,21},{6,22},{7,23},{8,24},{9,... | collective-permute-start | bytes 393224 | tf_op jit(solution)/shard_map/ppermute | solution.py:211
  26.9 11.7 %collective-permute-start.8 = (bf16[256,256]{1,0:T(8,128)(2,1)S(1)}, bf16[256,256]{1,0:T(8,128)(2,1)S(1)}, u32[]{:S(2)}, u32[]{:S(2)}) collective-permute-start(bf16[256,256]{1,0:T(8,128)(2,1)S(1)} %get-tuple-element.68), channel_id=1, source_target_pairs={{0,16},{1,17},{2,18},{3,19},{4,20},{5,21},{6,22},{7,23},{8,24},{9,... | collective-permute-start | bytes 393224 | tf_op jit(solution)/shard_map/ppermute | solution.py:211
  27.7 4.3 %collective-permute-start.6 = (bf16[128,256]{1,0:T(8,128)(2,1)S(1)}, bf16[128,256]{1,0:T(8,128)(2,1)S(1)}, u32[]{:S(2)}, u32[]{:S(2)}) collective-permute-start(bf16[128,256]{1,0:T(8,128)(2,1)S(1)} %get-tuple-element.66), channel_id=1, source_target_pairs={{0,1},{1,0},{2,3},{3,2},{4,5},{5,4},{6,7},{7,6},{8,9},{9,8},{10,11... | collective-permute-start | bytes 196616 | tf_op jit(solution)/shard_map/ppermute | solution.py:222
  27.7 8.1 %collective-permute-start.7 = (bf16[128,256]{1,0:T(8,128)(2,1)S(1)}, bf16[128,256]{1,0:T(8,128)(2,1)S(1)}, u32[]{:S(2)}, u32[]{:S(2)}) collective-permute-start(bf16[128,256]{1,0:T(8,128)(2,1)S(1)} %get-tuple-element.67), channel_id=1, source_target_pairs={{0,31},{1,2},{2,1},{3,4},{4,3},{5,6},{6,5},{7,8},{8,7},{9,10},{10,... | collective-permute-start | bytes 196616 | tf_op jit(solution)/shard_map/ppermute | solution.py:221
  29.6 14.9 %collective-permute-start.12 = (bf16[256,256]{1,0:T(8,128)(2,1)S(1)}, bf16[256,256]{1,0:T(8,128)(2,1)S(1)}, u32[]{:S(2)}, u32[]{:S(2)}) collective-permute-start(bf16[256,256]{1,0:T(8,128)(2,1)S(1)} %get-tuple-element.76), channel_id=1, source_target_pairs={{0,16},{1,17},{2,18},{3,19},{4,20},{5,21},{6,22},{7,23},{8,24},{9,... | collective-permute-start | bytes 393224 | tf_op jit(solution)/shard_map/ppermute | solution.py:211
  39.1 10.2 %collective-permute-start.11 = (bf16[256,256]{1,0:T(8,128)(2,1)S(1)}, bf16[256,256]{1,0:T(8,128)(2,1)S(1)}, u32[]{:S(2)}, u32[]{:S(2)}) collective-permute-start(bf16[256,256]{1,0:T(8,128)(2,1)S(1)} %get-tuple-element.73), channel_id=1, source_target_pairs={{0,16},{1,17},{2,18},{3,19},{4,20},{5,21},{6,22},{7,23},{8,24},{9,... | collective-permute-start | bytes 393224 | tf_op jit(solution)/shard_map/ppermute | solution.py:211
  42.0 4.6 %collective-permute-start.9 = (bf16[128,256]{1,0:T(8,128)(2,1)S(1)}, bf16[128,256]{1,0:T(8,128)(2,1)S(1)}, u32[]{:S(2)}, u32[]{:S(2)}) collective-permute-start(bf16[128,256]{1,0:T(8,128)(2,1)S(1)} %get-tuple-element.71), channel_id=1, source_target_pairs={{0,1},{1,0},{2,3},{3,2},{4,5},{5,4},{6,7},{7,6},{8,9},{9,8},{10,11... | collective-permute-start | bytes 196616 | tf_op jit(solution)/shard_map/ppermute | solution.py:222
  42.0 7.3 %collective-permute-start.10 = (bf16[128,256]{1,0:T(8,128)(2,1)S(1)}, bf16[128,256]{1,0:T(8,128)(2,1)S(1)}, u32[]{:S(2)}, u32[]{:S(2)}) collective-permute-start(bf16[128,256]{1,0:T(8,128)(2,1)S(1)} %get-tuple-element.72), channel_id=1, source_target_pairs={{0,31},{1,2},{2,1},{3,4},{4,3},{5,6},{6,5},{7,8},{8,7},{9,10},{10,... | collective-permute-start | bytes 196616 | tf_op jit(solution)/shard_map/ppermute | solution.py:221
  50.0 1.4 %collective-permute-start.13 = (f32[128,256]{1,0:T(8,128)S(1)}, f32[128,256]{1,0:T(8,128)S(1)}, u32[]{:S(2)}, u32[]{:S(2)}) collective-permute-start(f32[128,256]{1,0:T(8,128)S(1)} %get-tuple-element.81), channel_id=1, source_target_pairs={{0,1},{1,0},{2,3},{3,2},{4,5},{5,4},{6,7},{7,6},{8,9},{9,8},{10,11... | collective-permute-start | bytes 393224 | tf_op jit(solution)/shard_map/ppermute | solution.py:230
  51.5 4.1 %collective-permute-start.14 = (bf16[128,256]{1,0:T(8,128)(2,1)S(1)}, bf16[128,256]{1,0:T(8,128)(2,1)S(1)}, u32[]{:S(2)}, u32[]{:S(2)}) collective-permute-start(bf16[128,256]{1,0:T(8,128)(2,1)S(1)} %add_convert_fusion.3), channel_id=1, source_target_pairs={{0,3},{1,2},{2,1},{3,0},{4,7},{5,6},{6,5},{7,4},{8,11},{9,10},{10,... | collective-permute-start | bytes 196616 | tf_op jit(solution)/shard_map/ppermute | solution.py:234
  55.6 4.1 %collective-permute-start.15 = (bf16[128,256]{1,0:T(8,128)(2,1)S(1)}, bf16[128,256]{1,0:T(8,128)(2,1)S(1)}, u32[]{:S(2)}, u32[]{:S(2)}) collective-permute-start(bf16[128,256]{1,0:T(8,128)(2,1)S(1)} %add_convert_fusion.2), channel_id=1, source_target_pairs={{0,5},{1,4},{2,7},{3,6},{4,1},{5,0},{6,3},{7,2},{8,13},{9,12},{10,... | collective-permute-start | bytes 196616 | tf_op jit(solution)/shard_map/ppermute | solution.py:234
  59.8 4.1 %collective-permute-start.16 = (bf16[128,256]{1,0:T(8,128)(2,1)S(1)}, bf16[128,256]{1,0:T(8,128)(2,1)S(1)}, u32[]{:S(2)}, u32[]{:S(2)}) collective-permute-start(bf16[128,256]{1,0:T(8,128)(2,1)S(1)} %add_convert_fusion.1), channel_id=1, source_target_pairs={{0,9},{1,8},{2,11},{3,10},{4,13},{5,12},{6,15},{7,14},{8,1},{9,0},... | collective-permute-start | bytes 196616 | tf_op jit(solution)/shard_map/ppermute | solution.py:234
  63.9 6.0 %collective-permute-start.17 = (bf16[128,256]{1,0:T(8,128)(2,1)S(1)}, bf16[128,256]{1,0:T(8,128)(2,1)S(1)}, u32[]{:S(2)}, u32[]{:S(2)}) collective-permute-start(bf16[128,256]{1,0:T(8,128)(2,1)S(1)} %add_convert_fusion), channel_id=1, source_target_pairs={{0,17},{1,16},{2,19},{3,18},{4,21},{5,20},{6,23},{7,22},{8,25},{9,... | collective-permute-start | bytes 196616 | tf_op jit(solution)/shard_map/ppermute | solution.py:234
  70.0 1.5 %collective-permute-start.18 = (f32[128,256]{1,0:T(8,128)S(1)}, f32[128,256]{1,0:T(8,128)S(1)}, u32[]{:S(2)}, u32[]{:S(2)}) collective-permute-start(f32[128,256]{1,0:T(8,128)S(1)} %convert_add_fusion.total), channel_id=1, source_target_pairs={{0,1},{1,0},{2,3},{3,2},{4,5},{5,4},{6,7},{7,6},{8,9},{9,8},{10,11... | collective-permute-start | bytes 393224 | tf_op jit(solution)/shard_map/ppermute | solution.py:237

commit v3 on v2

--- a/solution.py
+++ b/solution.py
@@ -98,7 +98,7 @@
 def setup_body(
     dst_in, src_in, count, tiles, pick, grad, slopes, scaled, states,
     own, edge, pick_own, pick_edge, pick_grad, pick_slopes, local, pick_local,
-    back_own, back_near, back_far, back_wide, total, dst, src, sems,
+    back_own, back_near, back_far, back_wide_a, back_wide_b, total, dst, src, sems,
 ):
     pairs = ((dst_in, dst), (src_in, src))
     copies = [pltpu.make_async_copy(source, held, sems.at[n]) for n, (source, held) in enumerate(pairs)]
@@ -136,7 +136,8 @@
     back = mm_lhs_t(edge[...], states[...]).astype(BF)
     back_near[...] = back[:size]
     back_far[...] = back[size : 2 * size]
-    back_wide[...] = back[2 * size :]
+    back_wide_a[...] = back[2 * size : 3 * size]
+    back_wide_b[...] = back[3 * size :]
 
 
 def arrived(near, far, wide):
@@ -166,15 +167,16 @@
     return grad[...].astype(F32) + mm_rhs_t(mixed, weight[...])
 
 
-def own_body(near, far, wide, local, edge, grad, slopes, weight, own, pick_own, local_out, pick_local_out):
+def own_body(near, far, wide, local, edge, grad, slopes, weight, *rest):
     scaled = (slopes[...].astype(F32) * newest(near, far, wide, local, edge, grad, weight)).astype(BF)
-    local_out[...] = mm(own[...], scaled)
-    pick_local_out[...] = mm(pick_own[...], scaled)
-
-
-def back_body(near, far, wide, back_own, pick, high, low):
-    size = wide.shape[0] // 2
-    came = jnp.concatenate([near[size:, :], far[size:, :], wide[...]], axis=0)
+    matrices, outs = rest[: len(rest) // 2], rest[len(rest) // 2 :]
+    for matrix, out in zip(matrices, outs):
+        out[...] = mm(matrix[...], scaled)
+
+
+def back_body(near, far, wide_a, wide_b, back_own, pick, high, low):
+    size = wide_a.shape[0]
+    came = jnp.concatenate([near[size:, :], far[size:, :], wide_a[...], wide_b[...]], axis=0)
     value = (back_own[...] + mm_lhs_t(pick[...], came)).T
     top = value.astype(BF)
     high[...] = top
@@ -213,6 +215,11 @@
     return jnp.concatenate(
         [lax.ppermute(wide[:size], "dom", ahead), lax.ppermute(wide[size:], "dom", behind)], axis=0
     )
+
+
+def swap_list(rows, step):
+    count = lax.axis_size("dom")
+    return lax.ppermute(rows, "dom", [(p, (p + step) % count) for p in range(count)])
 
 
 def exchange(near, far, wide):
@@ -259,14 +266,14 @@
     came = exchange(near, far, wide)
     (
         own, edge, pick_own, pick_edge, pick_grad, pick_slopes, local, pick_local, back_own,
-        back_near, back_far, back_wide,
+        back_near, back_far, back_wide_a, back_wide_b,
     ) = call(
         setup_body,
         [
             ((rows, rows), BF), ((rows, cut), BF), ((cut, rows), BF), ((cut, cut), BF),
             ((cut, width), BF), ((cut, width), BF), (field, F32), ((cut, width), F32),
             (field, F32),
-        ] + message,
+        ] + [((size, width), BF)] * LISTS,
         "hhsvvvvvv",
         [
             pltpu.VMEM((blocks, rows, size), F32), pltpu.SMEM((slots,), jnp.int32),
@@ -274,20 +281,22 @@
         ],
     )(*in_hbm(tile_dst, tile_src), tile_count, tiles, pick, grad_out, slopes, scaled, states)
 
+    back_wide_a = swap_list(back_wide_a, -REACH)
+    back_wide_b = swap_list(back_wide_b, REACH)
+    pick_local = (pick_local,)
     for step in range(ITERS - 1):
         extra = (back_near, back_far) if step == 0 else ()
-        operands = (*came, pick_local, pick_edge, pick_grad, pick_slopes, weight, *extra)
+        operands = (*came, *pick_local, pick_edge, pick_grad, pick_slopes, weight, *extra)
         sent = call(send_body, longer if extra else message, "v" * len(operands))(*operands)
         following = exchange(*sent)
-        if step == 0:
-            back_wide = swap_wide(back_wide, False)
-        local, pick_local = call(own_body, [(field, F32), ((cut, width), F32)], "v" * 10)(
-            *came, local, edge, grad_out, slopes, weight, own, pick_own
+        matrices = (own, pick_own) if step < ITERS - 2 else (own,)
+        local, *pick_local = call(own_body, [((m.shape[0], width), F32) for m in matrices], "v" * (8 + len(matrices)))(
+            *came, local, edge, grad_out, slopes, weight, *matrices
         )
         came = following
         if step == 0:
-            back_came = (came[0], came[1], back_wide)
-    high, low = call(back_body, [((width, rows), BF), ((width, rows), BF)], "vvvvv")(*back_came, back_own, pick)
+            back_came = (came[0], came[1], back_wide_a, back_wide_b)
+    high, low = call(back_body, [((width, rows), BF), ((width, rows), BF)], "v" * 6)(*back_came, back_own, pick)
     factor = 1.0 / float(lax.axis_size("dom") * rows) ** 0.5
     half = ((width // 2, width), F32)
     kept, given = call(functools.partial(last_body, factor), [half, half], "v" * 10)(

time: 72.4 us -> 73.7 us (1.018)
  starting transfers between devices: 22.6 us -> 26.9 us
  waiting for transfers between devices: 36.3 us -> 34.1 us
  Pallas kernels: 11.7 us -> 10.9 us
    ppermute x0 -> x2, waiting for transfers between devices: none -> 5.84 us  [swap_list(): lax.ppermute(rows, 'dom', [(p, (p + step) % count) for p in range(count)])]
    ppermute x4, starting transfers between devices: 0.61 us -> 5.46 us  [summed(): lax.ppermute(mine, 'dom', [(p, p ^ step ^ 1) for p in range(count)])]
    ppermute x4, waiting for transfers between devices: 17.8 us -> 14.4 us  [summed(): lax.ppermute(mine, 'dom', [(p, p ^ step ^ 1) for p in range(count)])]
    ppermute x0 -> x2, starting transfers between devices: none -> 2.92 us  [swap_list(): lax.ppermute(rows, 'dom', [(p, (p + step) % count) for p in range(count)])]
    ppermute x5 -> x4, waiting for transfers between devices: 5.64 us -> 2.84 us  [swap_wide(): return lax.ppermute(wide, 'dom', ahead)]
    ppermute x4, starting transfers between devices: 12.3 us -> 10.4 us  [exchange(): lax.ppermute(far, 'dom', [(p, (p + 1 if p % 2 else p - 1) % count) for p...]
    ppermute x4, waiting for transfers between devices: 11.6 us -> 9.72 us  [exchange(): lax.ppermute(far, 'dom', [(p, (p + 1 if p % 2 else p - 1) % count) for p...]
    ppermute x5 -> x4, starting transfers between devices: 9.36 us -> 7.71 us  [swap_wide(): return lax.ppermute(wide, 'dom', ahead)]
  transfers between devices with their start and end apart: 19 -> 20, of which waited for: 11 -> 11; matrix products, arithmetic and copies ran while one was open for 0% -> 0% of each run, Pallas kernels for 11% -> 9%
where the time goes in v3:
time: 73.7 us; the launch traced here: 73.5 us
  waiting for transfers between devices  34.1 us (46%)
  starting transfers between devices  26.9 us (36%)
  Pallas kernels  10.9 us (15%)
  between operations  1.44 us (2%)
    ppermute x4, waiting for transfers between devices, summed(): lax.ppermute(mine, 'dom', [(p, p ^ step ^ 1) for p in range(count)])  14.4 us
    ppermute x4, starting transfers between devices, exchange(): lax.ppermute(far, 'dom', [(p, (p + 1 if p % 2 else p - 1) % count) for p...  10.4 us
    ppermute x4, waiting for transfers between devices, exchange(): lax.ppermute(far, 'dom', [(p, (p + 1 if p % 2 else p - 1) % count) for p...  9.72 us
    ppermute x4, starting transfers between devices, swap_wide(): return lax.ppermute(wide, 'dom', ahead)  7.71 us
    ppermute x2, waiting for transfers between devices, swap_list(): lax.ppermute(rows, 'dom', [(p, (p + step) % count) for p in range(count)])  5.84 us
    ppermute x4, starting transfers between devices, summed(): lax.ppermute(mine, 'dom', [(p, p ^ step ^ 1) for p in range(count)])  5.46 us
    ppermute x2, starting transfers between devices, swap_list(): lax.ppermute(rows, 'dom', [(p, (p + step) % count) for p in range(count)])  2.92 us
    ppermute x4, waiting for transfers between devices, swap_wide(): return lax.ppermute(wide, 'dom', ahead)  2.84 us
  transfers between devices with their start and end apart: 20, of which 11 were waited for; matrix products, arithmetic and copies ran while one was open for 0% of the time, Pallas kernels for 9%

profile of v3, /device:TPU:0, one launch (start us, length us, event | category | flops | bytes accessed | tf_op | source)
XLA Modules:
  0.0 73.5 jit_solution(13088089425902595014)
XLA Ops:
  0.6 1.4 %shard_map.104 = (bf16[128,256]{1,0:T(8,128)(2,1)S(1)}, bf16[128,256]{1,0:T(8,128)(2,1)S(1)}, bf16[256,256]{1,0:T(8,128)(2,1)S(1)}, bf16[512,256]{1,0:T(8,128)(2...) custom-call(s32[4,128]{1,0:T(4,128)} %lists_in.1, ...), custom_call_target="tpu_custom_call" | custom-call | tf_op jit(solution)/shard_map/pallas_call | solution.py:257
  2.1 4.1 %collective-permute-start.2 = (bf16[256,256]{1,0:T(8,128)(2,1)S(1)}, bf16[256,256]{1,0:T(8,128)(2,1)S(1)}, u32[]{:S(2)}, u32[]{:S(2)}) collective-permute-start(bf16[256,256]{1,0:T(8,128)(2,1)S(1)} %get-tuple-element.44), channel_id=1, source_target_pairs={{0,16},{1,17},{2,18},{3,19},{4,20},{5,21},{6,22},{7,23},{8,24},{9,... | collective-permute-start | bytes 393224 | tf_op jit(solution)/shard_map/ppermute | solution.py:213
  6.2 0.0 collective-permute-start
  6.2 3.3 %collective-permute-start.1 = (bf16[128,256]{1,0:T(8,128)(2,1)S(1)}, bf16[128,256]{1,0:T(8,128)(2,1)S(1)}, u32[]{:S(2)}, u32[]{:S(2)}) collective-permute-start(bf16[128,256]{1,0:T(8,128)(2,1)S(1)} %get-tuple-element.43), channel_id=1, source_target_pairs={{0,31},{1,2},{2,1},{3,4},{4,3},{5,6},{6,5},{7,8},{8,7},{9,10},{10,... | collective-permute-start | bytes 196616 | tf_op jit(solution)/shard_map/ppermute | solution.py:228
  10.2 2.3 %shard_map.105 = (bf16[512,512]{1,0:T(8,128)(2,1)S(1)}, bf16[512,512]{1,0:T(8,128)(2,1)S(1)}, bf16[512,512]{1,0:T(8,128)(2,1)S(1)}, bf16[512,512]{1,0:T(8,128)(2...) custom-call(s32[24]{0:T(128)} %dst_in.1, ...), custom_call_target="tpu_custom_call" | custom-call | tf_op jit(solution)/shard_map/pallas_call | solution.py:270
  12.5 0.0 collective-permute-done.near
  12.5 1.0 %collective-permute-done.1.far = bf16[128,256]{1,0:T(8,128)(2,1)S(1)} collective-permute-done((bf16[128,256]{1,0:T(8,128)(2,1)S(1)}, bf16[128,256]{1,0:T(8,128)(2,1)S(1)}, u32[]{:S(2)}, u32[]{:S(2)}) %collective-permute-start.1) | collective-permute-done | bytes 65568 | tf_op jit(solution)/shard_map/ppermute | solution.py:228
  13.5 0.5 shard_map.106
  14.0 0.1 collective-permute-start.3
  14.1 4.6 %collective-permute-start.4 = (bf16[256,256]{1,0:T(8,128)(2,1)S(1)}, bf16[256,256]{1,0:T(8,128)(2,1)S(1)}, u32[]{:S(2)}, u32[]{:S(2)}) collective-permute-start(bf16[256,256]{1,0:T(8,128)(2,1)S(1)} %get-tuple-element.59), channel_id=1, source_target_pairs={{0,31},{1,2},{2,1},{3,4},{4,3},{5,6},{6,5},{7,8},{8,7},{9,10},{10,... | collective-permute-start | bytes 393224 | tf_op jit(solution)/shard_map/ppermute | solution.py:228
  18.7 0.0 collective-permute-start.5
  18.7 0.8 %shard_map.107 = (f32[512,256]{1,0:T(8,128)S(1)}, f32[512,256]{1,0:T(8,128)S(1)}) custom-call(bf16[128,256]{1,0:T(8,128)(2,1)S(1)} %collective-permute-done.near, bf16[128,256]{1,0:T(8,128)(2,1)S(1)} %collective-permute-done.1.far, bf16[256,256]{1,0:T(8,128)(2,1)S(1)} %collective-permute-done.2.wide, f32[512,256]{1,0:T(8,128)S(1)} %get-tuple-element.61.local, ...), custom_call_target="tpu_custom_call" | custom-call | tf_op jit(solution)/shard_map/pallas_call | solution.py:293
  19.6 4.0 %collective-permute-done.4.far = bf16[256,256]{1,0:T(8,128)(2,1)S(1)} collective-permute-done((bf16[256,256]{1,0:T(8,128)(2,1)S(1)}, bf16[256,256]{1,0:T(8,128)(2,1)S(1)}, u32[]{:S(2)}, u32[]{:S(2)}) %collective-permute-start.4) | collective-permute-done | bytes 131104 | tf_op jit(solution)/shard_map/ppermute | solution.py:228
  23.6 2.8 %collective-permute-done.5.wide = bf16[256,256]{1,0:T(8,128)(2,1)S(1)} collective-permute-done((bf16[256,256]{1,0:T(8,128)(2,1)S(1)}, bf16[256,256]{1,0:T(8,128)(2,1)S(1)}, u32[]{:S(2)}, u32[]{:S(2)}) %collective-permute-start.5) | collective-permute-done | bytes 131104 | tf_op jit(solution)/shard_map/ppermute | solution.py:213
  26.4 0.5 shard_map.108
  26.9 0.8 %collective-permute-start.8 = (bf16[256,256]{1,0:T(8,128)(2,1)S(1)}, bf16[256,256]{1,0:T(8,128)(2,1)S(1)}, u32[]{:S(2)}, u32[]{:S(2)}) collective-permute-start(bf16[256,256]{1,0:T(8,128)(2,1)S(1)} %get-tuple-element.68), channel_id=1, source_target_pairs={{0,16},{1,17},{2,18},{3,19},{4,20},{5,21},{6,22},{7,23},{8,24},{9,... | collective-permute-start | bytes 393224 | tf_op jit(solution)/shard_map/ppermute | solution.py:213
  27.7 0.0 collective-permute-start.6
  27.7 1.9 %collective-permute-start.7 = (bf16[128,256]{1,0:T(8,128)(2,1)S(1)}, bf16[128,256]{1,0:T(8,128)(2,1)S(1)}, u32[]{:S(2)}, u32[]{:S(2)}) collective-permute-start(bf16[128,256]{1,0:T(8,128)(2,1)S(1)} %get-tuple-element.67), channel_id=1, source_target_pairs={{0,31},{1,2},{2,1},{3,4},{4,3},{5,6},{6,5},{7,8},{8,7},{9,10},{10,... | collective-permute-start | bytes 196616 | tf_op jit(solution)/shard_map/ppermute | solution.py:228
  29.6 0.8 %shard_map.109 = (f32[512,256]{1,0:T(8,128)S(1)}, f32[512,256]{1,0:T(8,128)S(1)}) custom-call(bf16[256,256]{1,0:T(8,128)(2,1)S(1)} %collective-permute-done.3.near, bf16[256,256]{1,0:T(8,128)(2,1)S(1)} %collective-permute-done.4.far, bf16[256,256]{1,0:T(8,128)(2,1)S(1)} %collective-permute-done.5.wide, f32[512,256]{1,0:T(8,128)S(1)} %get-tuple-element.69.local, ...), custom_call_target="tpu_custom_call" | custom-call | tf_op jit(solution)/shard_map/pallas_call | solution.py:293
  30.4 0.0 collective-permute-done.6.near
  30.5 4.7 %collective-permute-done.7.far = bf16[128,256]{1,0:T(8,128)(2,1)S(1)} collective-permute-done((bf16[128,256]{1,0:T(8,128)(2,1)S(1)}, bf16[128,256]{1,0:T(8,128)(2,1)S(1)}, u32[]{:S(2)}, u32[]{:S(2)}) %collective-permute-start.7) | collective-permute-done | bytes 65568 | tf_op jit(solution)/shard_map/ppermute | solution.py:228
  35.1 0.5 shard_map.110
  35.6 2.8 %collective-permute-start.11 = (bf16[256,256]{1,0:T(8,128)(2,1)S(1)}, bf16[256,256]{1,0:T(8,128)(2,1)S(1)}, u32[]{:S(2)}, u32[]{:S(2)}) collective-permute-start(bf16[256,256]{1,0:T(8,128)(2,1)S(1)} %get-tuple-element.73), channel_id=1, source_target_pairs={{0,16},{1,17},{2,18},{3,19},{4,20},{5,21},{6,22},{7,23},{8,24},{9,... | collective-permute-start | bytes 393224 | tf_op jit(solution)/shard_map/ppermute | solution.py:213
  38.4 0.2 collective-permute-start.12
  38.6 2.7 %collective-permute-start.13 = (bf16[128,256]{1,0:T(8,128)(2,1)S(1)}, bf16[128,256]{1,0:T(8,128)(2,1)S(1)}, u32[]{:S(2)}, u32[]{:S(2)}) collective-permute-start(bf16[128,256]{1,0:T(8,128)(2,1)S(1)} %get-tuple-element.76), channel_id=1, source_target_pairs={{0,16},{1,17},{2,18},{3,19},{4,20},{5,21},{6,22},{7,23},{8,24},{9,... | collective-permute-start | bytes 196616 | tf_op jit(solution)/shard_map/ppermute | solution.py:222
  41.4 0.0 collective-permute-start.9
  41.4 0.6 collective-permute-start.10
  41.9 5.1 %collective-permute-done.12.wide_a = bf16[128,256]{1,0:T(8,128)(2,1)S(1)} collective-permute-done((bf16[128,256]{1,0:T(8,128)(2,1)S(1)}, bf16[128,256]{1,0:T(8,128)(2,1)S(1)}, u32[]{:S(2)}, u32[]{:S(2)}) %collective-permute-start.12) | collective-permute-done | bytes 65568 | tf_op jit(solution)/shard_map/ppermute | solution.py:222
  47.1 0.7 collective-permute-done.13.wide_b
  47.8 0.4 shard_map.113
  48.2 0.9 %shard_map.111.local = f32[512,256]{1,0:T(8,128)S(1)} custom-call(bf16[128,256]{1,0:T(8,128)(2,1)S(1)} %collective-permute-done.6.near, bf16[128,256]{1,0:T(8,128)(2,1)S(1)} %collective-permute-done.7.far, bf16[256,256]{1,0:T(8,128)(2,1)S(1)} %collective-permute-done.8.wide, f32[512,256]{1,0:T(8,128)S(1)} %get-tuple-element.74.local, ...), custom_call_target="tpu_custom_call" | custom-call | tf_op jit(solution)/shard_map/pallas_call | solution.py:293
  49.1 0.0 collective-permute-done.9.near
  49.1 0.0 collective-permute-done.10.far
  49.1 0.8 %shard_map.114 = (f32[128,256]{1,0:T(8,128)S(1)}, f32[128,256]{1,0:T(8,128)S(1)}) custom-call(bf16[128,256]{1,0:T(8,128)(2,1)S(1)} %collective-permute-done.9.near, bf16[128,256]{1,0:T(8,128)(2,1)S(1)} %collective-permute-done.10.far, bf16[256,256]{1,0:T(8,128)(2,1)S(1)} %collective-permute-done.11.wide, f32[512,256]{1,0:T(8,128)S(1)} %shard_map.111.local, ...), custom_call_target="tpu_custom_call" | custom-call | tf_op jit(solution)/shard_map/pallas_call | solution.py:302
  49.9 0.1 collective-permute-start.14
  50.0 1.3 %collective-permute-done.14 = f32[128,256]{1,0:T(8,128)S(1)} collective-permute-done((f32[128,256]{1,0:T(8,128)S(1)}, f32[128,256]{1,0:T(8,128)S(1)}, u32[]{:S(2)}, u32[]{:S(2)}) %collective-permute-start.14) | collective-permute-done | bytes 131104 | tf_op jit(solution)/shard_map/ppermute | solution.py:237
  51.3 0.2 collective-permute-start.15
  51.6 3.9 %collective-permute-done.15 = bf16[128,256]{1,0:T(8,128)(2,1)S(1)} collective-permute-done((bf16[128,256]{1,0:T(8,128)(2,1)S(1)}, bf16[128,256]{1,0:T(8,128)(2,1)S(1)}, u32[]{:S(2)}, u32[]{:S(2)}) %collective-permute-start.15) | collective-permute-done | bytes 65568 | tf_op jit(solution)/shard_map/ppermute | solution.py:241
  55.5 3.2 %collective-permute-start.16 = (bf16[128,256]{1,0:T(8,128)(2,1)S(1)}, bf16[128,256]{1,0:T(8,128)(2,1)S(1)}, u32[]{:S(2)}, u32[]{:S(2)}) collective-permute-start(bf16[128,256]{1,0:T(8,128)(2,1)S(1)} %add_convert_fusion.2), channel_id=1, source_target_pairs={{0,5},{1,4},{2,7},{3,6},{4,1},{5,0},{6,3},{7,2},{8,13},{9,12},{10,... | collective-permute-start | bytes 196616 | tf_op jit(solution)/shard_map/ppermute | solution.py:241
  58.7 2.3 %collective-permute-done.16 = bf16[128,256]{1,0:T(8,128)(2,1)S(1)} collective-permute-done((bf16[128,256]{1,0:T(8,128)(2,1)S(1)}, bf16[128,256]{1,0:T(8,128)(2,1)S(1)}, u32[]{:S(2)}, u32[]{:S(2)}) %collective-permute-start.16) | collective-permute-done | bytes 65568 | tf_op jit(solution)/shard_map/ppermute | solution.py:241
  61.0 0.1 collective-permute-start.17
  61.1 4.0 %collective-permute-done.17 = bf16[128,256]{1,0:T(8,128)(2,1)S(1)} collective-permute-done((bf16[128,256]{1,0:T(8,128)(2,1)S(1)}, bf16[128,256]{1,0:T(8,128)(2,1)S(1)}, u32[]{:S(2)}, u32[]{:S(2)}) %collective-permute-start.17) | collective-permute-done | bytes 65568 | tf_op jit(solution)/shard_map/ppermute | solution.py:241
  65.1 1.9 %collective-permute-start.18 = (bf16[128,256]{1,0:T(8,128)(2,1)S(1)}, bf16[128,256]{1,0:T(8,128)(2,1)S(1)}, u32[]{:S(2)}, u32[]{:S(2)}) collective-permute-start(bf16[128,256]{1,0:T(8,128)(2,1)S(1)} %add_convert_fusion), channel_id=1, source_target_pairs={{0,17},{1,16},{2,19},{3,18},{4,21},{5,20},{6,23},{7,22},{8,25},{9,... | collective-permute-start | bytes 196616 | tf_op jit(solution)/shard_map/ppermute | solution.py:241
  67.0 4.2 %collective-permute-done.18 = bf16[128,256]{1,0:T(8,128)(2,1)S(1)} collective-permute-done((bf16[128,256]{1,0:T(8,128)(2,1)S(1)}, bf16[128,256]{1,0:T(8,128)(2,1)S(1)}, u32[]{:S(2)}, u32[]{:S(2)}) %collective-permute-start.18) | collective-permute-done | bytes 65568 | tf_op jit(solution)/shard_map/ppermute | solution.py:241
  71.3 0.2 collective-permute-start.19
  71.4 1.3 %shard_map.112 = f32[512,256]{1,0:T(8,128)} custom-call(bf16[128,256]{1,0:T(8,128)(2,1)S(1)} %collective-permute-done.9.near, bf16[128,256]{1,0:T(8,128)(2,1)S(1)} %collective-permute-done.10.far, bf16[256,256]{1,0:T(8,128)(2,1)S(1)} %collective-permute-done.11.wide, f32[512,256]{1,0:T(8,128)S(1)} %shard_map.111.local, ...), custom_call_target="tpu_custom_call" | custom-call | tf_op jit(solution)/shard_map/pallas_call | solution.py:305
  72.7 0.0 collective-permute-done.19.other
  72.7 0.7 shard_map.115
  (9 shorter events, 0.1 us)
Async XLA Ops:
  2.1 11.4 %collective-permute-start.2 = (bf16[256,256]{1,0:T(8,128)(2,1)S(1)}, bf16[256,256]{1,0:T(8,128)(2,1)S(1)}, u32[]{:S(2)}, u32[]{:S(2)}) collective-permute-start(bf16[256,256]{1,0:T(8,128)(2,1)S(1)} %get-tuple-element.44), channel_id=1, source_target_pairs={{0,16},{1,17},{2,18},{3,19},{4,20},{5,21},{6,22},{7,23},{8,24},{9,... | collective-permute-start | bytes 393224 | tf_op jit(solution)/shard_map/ppermute | solution.py:213
  6.2 6.3 %collective-permute-start = (bf16[128,256]{1,0:T(8,128)(2,1)S(1)}, bf16[128,256]{1,0:T(8,128)(2,1)S(1)}, u32[]{:S(2)}, u32[]{:S(2)}) collective-permute-start(bf16[128,256]{1,0:T(8,128)(2,1)S(1)} %get-tuple-element.42), channel_id=1, source_target_pairs={{0,1},{1,0},{2,3},{3,2},{4,5},{5,4},{6,7},{7,6},{8,9},{9,8},{10,11... | collective-permute-start | bytes 196616 | tf_op jit(solution)/shard_map/ppermute | solution.py:229
  6.2 7.3 %collective-permute-start.1 = (bf16[128,256]{1,0:T(8,128)(2,1)S(1)}, bf16[128,256]{1,0:T(8,128)(2,1)S(1)}, u32[]{:S(2)}, u32[]{:S(2)}) collective-permute-start(bf16[128,256]{1,0:T(8,128)(2,1)S(1)} %get-tuple-element.43), channel_id=1, source_target_pairs={{0,31},{1,2},{2,1},{3,4},{4,3},{5,6},{6,5},{7,8},{8,7},{9,10},{10,... | collective-permute-start | bytes 196616 | tf_op jit(solution)/shard_map/ppermute | solution.py:228
  14.0 5.5 %collective-permute-start.3 = (bf16[256,256]{1,0:T(8,128)(2,1)S(1)}, bf16[256,256]{1,0:T(8,128)(2,1)S(1)}, u32[]{:S(2)}, u32[]{:S(2)}) collective-permute-start(bf16[256,256]{1,0:T(8,128)(2,1)S(1)} %get-tuple-element.58), channel_id=1, source_target_pairs={{0,1},{1,0},{2,3},{3,2},{4,5},{5,4},{6,7},{7,6},{8,9},{9,8},{10,11... | collective-permute-start | bytes 393224 | tf_op jit(solution)/shard_map/ppermute | solution.py:229
  14.1 9.5 %collective-permute-start.4 = (bf16[256,256]{1,0:T(8,128)(2,1)S(1)}, bf16[256,256]{1,0:T(8,128)(2,1)S(1)}, u32[]{:S(2)}, u32[]{:S(2)}) collective-permute-start(bf16[256,256]{1,0:T(8,128)(2,1)S(1)} %get-tuple-element.59), channel_id=1, source_target_pairs={{0,31},{1,2},{2,1},{3,4},{4,3},{5,6},{6,5},{7,8},{8,7},{9,10},{10,... | collective-permute-start | bytes 393224 | tf_op jit(solution)/shard_map/ppermute | solution.py:228
  18.7 7.7 %collective-permute-start.5 = (bf16[256,256]{1,0:T(8,128)(2,1)S(1)}, bf16[256,256]{1,0:T(8,128)(2,1)S(1)}, u32[]{:S(2)}, u32[]{:S(2)}) collective-permute-start(bf16[256,256]{1,0:T(8,128)(2,1)S(1)} %get-tuple-element.60), channel_id=1, source_target_pairs={{0,16},{1,17},{2,18},{3,19},{4,20},{5,21},{6,22},{7,23},{8,24},{9,... | collective-permute-start | bytes 393224 | tf_op jit(solution)/shard_map/ppermute | solution.py:213
  26.9 8.2 %collective-permute-start.8 = (bf16[256,256]{1,0:T(8,128)(2,1)S(1)}, bf16[256,256]{1,0:T(8,128)(2,1)S(1)}, u32[]{:S(2)}, u32[]{:S(2)}) collective-permute-start(bf16[256,256]{1,0:T(8,128)(2,1)S(1)} %get-tuple-element.68), channel_id=1, source_target_pairs={{0,16},{1,17},{2,18},{3,19},{4,20},{5,21},{6,22},{7,23},{8,24},{9,... | collective-permute-start | bytes 393224 | tf_op jit(solution)/shard_map/ppermute | solution.py:213
  27.7 2.7 %collective-permute-start.6 = (bf16[128,256]{1,0:T(8,128)(2,1)S(1)}, bf16[128,256]{1,0:T(8,128)(2,1)S(1)}, u32[]{:S(2)}, u32[]{:S(2)}) collective-permute-start(bf16[128,256]{1,0:T(8,128)(2,1)S(1)} %get-tuple-element.66), channel_id=1, source_target_pairs={{0,1},{1,0},{2,3},{3,2},{4,5},{5,4},{6,7},{7,6},{8,9},{9,8},{10,11... | collective-permute-start | bytes 196616 | tf_op jit(solution)/shard_map/ppermute | solution.py:229
  27.7 7.4 %collective-permute-start.7 = (bf16[128,256]{1,0:T(8,128)(2,1)S(1)}, bf16[128,256]{1,0:T(8,128)(2,1)S(1)}, u32[]{:S(2)}, u32[]{:S(2)}) collective-permute-start(bf16[128,256]{1,0:T(8,128)(2,1)S(1)} %get-tuple-element.67), channel_id=1, source_target_pairs={{0,31},{1,2},{2,1},{3,4},{4,3},{5,6},{6,5},{7,8},{8,7},{9,10},{10,... | collective-permute-start | bytes 196616 | tf_op jit(solution)/shard_map/ppermute | solution.py:228
  35.6 13.5 %collective-permute-start.11 = (bf16[256,256]{1,0:T(8,128)(2,1)S(1)}, bf16[256,256]{1,0:T(8,128)(2,1)S(1)}, u32[]{:S(2)}, u32[]{:S(2)}) collective-permute-start(bf16[256,256]{1,0:T(8,128)(2,1)S(1)} %get-tuple-element.73), channel_id=1, source_target_pairs={{0,16},{1,17},{2,18},{3,19},{4,20},{5,21},{6,22},{7,23},{8,24},{9,... | collective-permute-start | bytes 393224 | tf_op jit(solution)/shard_map/ppermute | solution.py:213
  38.4 8.7 %collective-permute-start.12 = (bf16[128,256]{1,0:T(8,128)(2,1)S(1)}, bf16[128,256]{1,0:T(8,128)(2,1)S(1)}, u32[]{:S(2)}, u32[]{:S(2)}) collective-permute-start(bf16[128,256]{1,0:T(8,128)(2,1)S(1)} %get-tuple-element.75), channel_id=1, source_target_pairs={{0,16},{1,17},{2,18},{3,19},{4,20},{5,21},{6,22},{7,23},{8,24},{9,... | collective-permute-start | bytes 196616 | tf_op jit(solution)/shard_map/ppermute | solution.py:222
  38.6 9.2 %collective-permute-start.13 = (bf16[128,256]{1,0:T(8,128)(2,1)S(1)}, bf16[128,256]{1,0:T(8,128)(2,1)S(1)}, u32[]{:S(2)}, u32[]{:S(2)}) collective-permute-start(bf16[128,256]{1,0:T(8,128)(2,1)S(1)} %get-tuple-element.76), channel_id=1, source_target_pairs={{0,16},{1,17},{2,18},{3,19},{4,20},{5,21},{6,22},{7,23},{8,24},{9,... | collective-permute-start | bytes 196616 | tf_op jit(solution)/shard_map/ppermute | solution.py:222
  41.4 7.7 %collective-permute-start.9 = (bf16[128,256]{1,0:T(8,128)(2,1)S(1)}, bf16[128,256]{1,0:T(8,128)(2,1)S(1)}, u32[]{:S(2)}, u32[]{:S(2)}) collective-permute-start(bf16[128,256]{1,0:T(8,128)(2,1)S(1)} %get-tuple-element.71), channel_id=1, source_target_pairs={{0,1},{1,0},{2,3},{3,2},{4,5},{5,4},{6,7},{7,6},{8,9},{9,8},{10,11... | collective-permute-start | bytes 196616 | tf_op jit(solution)/shard_map/ppermute | solution.py:229
  41.4 7.8 %collective-permute-start.10 = (bf16[128,256]{1,0:T(8,128)(2,1)S(1)}, bf16[128,256]{1,0:T(8,128)(2,1)S(1)}, u32[]{:S(2)}, u32[]{:S(2)}) collective-permute-start(bf16[128,256]{1,0:T(8,128)(2,1)S(1)} %get-tuple-element.72), channel_id=1, source_target_pairs={{0,31},{1,2},{2,1},{3,4},{4,3},{5,6},{6,5},{7,8},{8,7},{9,10},{10,... | collective-permute-start | bytes 196616 | tf_op jit(solution)/shard_map/ppermute | solution.py:228
  49.9 1.4 %collective-permute-start.14 = (f32[128,256]{1,0:T(8,128)S(1)}, f32[128,256]{1,0:T(8,128)S(1)}, u32[]{:S(2)}, u32[]{:S(2)}) collective-permute-start(f32[128,256]{1,0:T(8,128)S(1)} %get-tuple-element.81), channel_id=1, source_target_pairs={{0,1},{1,0},{2,3},{3,2},{4,5},{5,4},{6,7},{7,6},{8,9},{9,8},{10,11... | collective-permute-start | bytes 393224 | tf_op jit(solution)/shard_map/ppermute | solution.py:237
  51.3 4.1 %collective-permute-start.15 = (bf16[128,256]{1,0:T(8,128)(2,1)S(1)}, bf16[128,256]{1,0:T(8,128)(2,1)S(1)}, u32[]{:S(2)}, u32[]{:S(2)}) collective-permute-start(bf16[128,256]{1,0:T(8,128)(2,1)S(1)} %add_convert_fusion.3), channel_id=1, source_target_pairs={{0,3},{1,2},{2,1},{3,0},{4,7},{5,6},{6,5},{7,4},{8,11},{9,10},{10,... | collective-permute-start | bytes 196616 | tf_op jit(solution)/shard_map/ppermute | solution.py:241
  55.5 5.5 %collective-permute-start.16 = (bf16[128,256]{1,0:T(8,128)(2,1)S(1)}, bf16[128,256]{1,0:T(8,128)(2,1)S(1)}, u32[]{:S(2)}, u32[]{:S(2)}) collective-permute-start(bf16[128,256]{1,0:T(8,128)(2,1)S(1)} %add_convert_fusion.2), channel_id=1, source_target_pairs={{0,5},{1,4},{2,7},{3,6},{4,1},{5,0},{6,3},{7,2},{8,13},{9,12},{10,... | collective-permute-start | bytes 196616 | tf_op jit(solution)/shard_map/ppermute | solution.py:241
  61.0 4.1 %collective-permute-start.17 = (bf16[128,256]{1,0:T(8,128)(2,1)S(1)}, bf16[128,256]{1,0:T(8,128)(2,1)S(1)}, u32[]{:S(2)}, u32[]{:S(2)}) collective-permute-start(bf16[128,256]{1,0:T(8,128)(2,1)S(1)} %add_convert_fusion.1), channel_id=1, source_target_pairs={{0,9},{1,8},{2,11},{3,10},{4,13},{5,12},{6,15},{7,14},{8,1},{9,0},... | collective-permute-start | bytes 196616 | tf_op jit(solution)/shard_map/ppermute | solution.py:241
  65.1 6.1 %collective-permute-start.18 = (bf16[128,256]{1,0:T(8,128)(2,1)S(1)}, bf16[128,256]{1,0:T(8,128)(2,1)S(1)}, u32[]{:S(2)}, u32[]{:S(2)}) collective-permute-start(bf16[128,256]{1,0:T(8,128)(2,1)S(1)} %add_convert_fusion), channel_id=1, source_target_pairs={{0,17},{1,16},{2,19},{3,18},{4,21},{5,20},{6,23},{7,22},{8,25},{9,... | collective-permute-start | bytes 196616 | tf_op jit(solution)/shard_map/ppermute | solution.py:241
  71.3 1.5 %collective-permute-start.19 = (f32[128,256]{1,0:T(8,128)S(1)}, f32[128,256]{1,0:T(8,128)S(1)}, u32[]{:S(2)}, u32[]{:S(2)}) collective-permute-start(f32[128,256]{1,0:T(8,128)S(1)} %convert_add_fusion.total), channel_id=1, source_target_pairs={{0,1},{1,0},{2,3},{3,2},{4,5},{5,4},{6,7},{7,6},{8,9},{9,8},{10,11... | collective-permute-start | bytes 393224 | tf_op jit(solution)/shard_map/ppermute | solution.py:244

commit v4 on v3

--- a/solution.py
+++ b/solution.py
@@ -16,13 +16,13 @@
 VMEM_BYTES = 8 * 1024 * 1024
 
 
-def call(body, outs, ins, scratch=()):
+def call(body, outs, ins, scratch=(), out_space=pltpu.VMEM):
     spaces = {"v": pltpu.VMEM, "s": pltpu.SMEM, "h": pltpu.HBM}
     return pl.pallas_call(
         body,
         out_shape=tuple(jax.ShapeDtypeStruct(shape, dtype) for shape, dtype in outs),
         in_specs=[pl.BlockSpec(memory_space=spaces[kind]) for kind in ins],
-        out_specs=tuple(pl.BlockSpec(memory_space=pltpu.VMEM) for _ in outs),
+        out_specs=tuple(pl.BlockSpec(memory_space=out_space) for _ in outs),
         scratch_shapes=list(scratch),
         compiler_params=pltpu.CompilerParams(vmem_limit_bytes=VMEM_BYTES),
     )
@@ -196,11 +196,17 @@
     out[...] = newest(near, far, wide, local, edge, grad, weight)
 
 
-def join_body(total, other, out):
+def join_body(total, other, out, sems):
     rows = total.shape[0]
     at = side()
-    out[pl.ds(pl.multiple_of(at * rows, rows), rows), :] = total[...]
-    out[pl.ds(pl.multiple_of((1 - at) * rows, rows), rows), :] = other[...]
+    copies = [
+        pltpu.make_async_copy(held, out.at[pl.ds(pl.multiple_of(half * rows, rows), rows), :], sems.at[n])
+        for n, (half, held) in enumerate(((at, total), (1 - at, other)))
+    ]
+    for copy in copies:
+        copy.start()
+    for copy in copies:
+        copy.wait()
 
 
 def swap_wide(wide, forward=True):
@@ -235,14 +241,18 @@
     rows, width = kept.shape
     beside = [(p, p ^ 1) for p in range(count)]
     total = kept + lax.ppermute(given, "dom", beside)
-    step = 2
-    while step < count:
+    for step in [1 << b for b in range(count.bit_length() - 2, 0, -1)]:
         mine = total.astype(BF)
-        theirs = lax.ppermute(mine, "dom", [(p, p ^ step ^ 1) for p in range(count)])
-        total = mine.astype(F32) + theirs.astype(F32)
-        step *= 2
+        pairs = [(p, p ^ step ^ 1) for p in range(count)]
+        parts = 2 if 2 * step == count else 1
+        theirs = []
+        for n in range(parts):
+            theirs.append(lax.ppermute(mine[n * rows // parts : (n + 1) * rows // parts], "dom", pairs))
+        total = mine.astype(F32) + jnp.concatenate(theirs, axis=0).astype(F32)
     other = lax.ppermute(total, "dom", beside)
-    return call(join_body, [((2 * rows, width), F32)], "vv")(total, other)[0]
+    return call(
+        join_body, [((2 * rows, width), F32)], "vv", [pltpu.SemaphoreType.DMA((2,))], pltpu.HBM
+    )(total, other)[0]
 
 
 def per_device(grad_out, states, slopes, weight, tiles, tile_dst, tile_src, tile_count, send_rows):

time: 73.7 us -> 74.6 us (1.012)
  waiting for transfers between devices: 34.1 us -> 36.5 us
  starting transfers between devices: 26.9 us -> 25.4 us
    ppermute x4 -> x5, waiting for transfers between devices: 14.4 us -> 16.8 us  [summed(): lax.ppermute(mine[n * rows // parts:(n + 1) * rows // parts], 'dom', pairs)]
    ppermute x4 -> x5, starting transfers between devices: 5.46 us -> 4.02 us  [summed(): lax.ppermute(mine[n * rows // parts:(n + 1) * rows // parts], 'dom', pairs)]
  transfers between devices with their start and end apart: 20 -> 21, of which waited for: 11 -> 12; matrix products, arithmetic and copies ran while one was open for 0% -> 0% of each run, Pallas kernels for 9% -> 9%
where the time goes in v4:
time: 74.6 us; the launch traced here: 74.4 us
  waiting for transfers between devices  36.5 us (49%)
  starting transfers between devices  25.4 us (34%)
  Pallas kernels  10.9 us (15%)
  between operations  1.46 us (2%)
    ppermute x5, waiting for transfers between devices, summed(): lax.ppermute(mine[n * rows // parts:(n + 1) * rows // parts], 'dom', pairs)  16.8 us
    ppermute x4, starting transfers between devices, exchange(): lax.ppermute(far, 'dom', [(p, (p + 1 if p % 2 else p - 1) % count) for p...  10.4 us
    ppermute x4, waiting for transfers between devices, exchange(): lax.ppermute(far, 'dom', [(p, (p + 1 if p % 2 else p - 1) % count) for p...  9.72 us
    ppermute x4, starting transfers between devices, swap_wide(): return lax.ppermute(wide, 'dom', ahead)  7.71 us
    ppermute x2, waiting for transfers between devices, swap_list(): lax.ppermute(rows, 'dom', [(p, (p + step) % count) for p in range(count)])  5.84 us
    ppermute x5, starting transfers between devices, summed(): lax.ppermute(mine[n * rows // parts:(n + 1) * rows // parts], 'dom', pairs)  4.02 us
    ppermute x2, starting transfers between devices, swap_list(): lax.ppermute(rows, 'dom', [(p, (p + step) % count) for p in range(count)])  2.92 us
    ppermute x4, waiting for transfers between devices, swap_wide(): return lax.ppermute(wide, 'dom', ahead)  2.84 us
  transfers between devices with their start and end apart: 21, of which 12 were waited for; matrix products, arithmetic and copies ran while one was open for 0% of the time, Pallas kernels for 9%

profile of v4, /device:TPU:0, one launch (start us, length us, event | category | flops | bytes accessed | tf_op | source)
XLA Modules:
  0.0 74.4 jit_solution(15326967805630365636)
XLA Ops:
  0.6 1.4 %shard_map.104 = (bf16[128,256]{1,0:T(8,128)(2,1)S(1)}, bf16[128,256]{1,0:T(8,128)(2,1)S(1)}, bf16[256,256]{1,0:T(8,128)(2,1)S(1)}, bf16[512,256]{1,0:T(8,128)(2...) custom-call(s32[4,128]{1,0:T(4,128)} %lists_in.1, ...), custom_call_target="tpu_custom_call" | custom-call | tf_op jit(solution)/shard_map/pallas_call | solution.py:267
  2.1 4.1 %collective-permute-start.2 = (bf16[256,256]{1,0:T(8,128)(2,1)S(1)}, bf16[256,256]{1,0:T(8,128)(2,1)S(1)}, u32[]{:S(2)}, u32[]{:S(2)}) collective-permute-start(bf16[256,256]{1,0:T(8,128)(2,1)S(1)} %get-tuple-element.44), channel_id=1, source_target_pairs={{0,16},{1,17},{2,18},{3,19},{4,20},{5,21},{6,22},{7,23},{8,24},{9,... | collective-permute-start | bytes 393224 | tf_op jit(solution)/shard_map/ppermute | solution.py:219
  6.2 3.3 %collective-permute-start.1 = (bf16[128,256]{1,0:T(8,128)(2,1)S(1)}, bf16[128,256]{1,0:T(8,128)(2,1)S(1)}, u32[]{:S(2)}, u32[]{:S(2)}) collective-permute-start(bf16[128,256]{1,0:T(8,128)(2,1)S(1)} %get-tuple-element.43), channel_id=1, source_target_pairs={{0,31},{1,2},{2,1},{3,4},{4,3},{5,6},{6,5},{7,8},{8,7},{9,10},{10,... | collective-permute-start | bytes 196616 | tf_op jit(solution)/shard_map/ppermute | solution.py:234
  10.2 2.3 %shard_map.105 = (bf16[512,512]{1,0:T(8,128)(2,1)S(1)}, bf16[512,512]{1,0:T(8,128)(2,1)S(1)}, bf16[512,512]{1,0:T(8,128)(2,1)S(1)}, bf16[512,512]{1,0:T(8,128)(2...) custom-call(s32[24]{0:T(128)} %dst_in.1, ...), custom_call_target="tpu_custom_call" | custom-call | tf_op jit(solution)/shard_map/pallas_call | solution.py:280
  12.5 0.0 collective-permute-done.near
  12.5 1.0 %collective-permute-done.1.far = bf16[128,256]{1,0:T(8,128)(2,1)S(1)} collective-permute-done((bf16[128,256]{1,0:T(8,128)(2,1)S(1)}, bf16[128,256]{1,0:T(8,128)(2,1)S(1)}, u32[]{:S(2)}, u32[]{:S(2)}) %collective-permute-start.1) | collective-permute-done | bytes 65568 | tf_op jit(solution)/shard_map/ppermute | solution.py:234
  13.5 0.5 shard_map.106
  14.0 0.1 collective-permute-start.3
  14.1 4.6 %collective-permute-start.4 = (bf16[256,256]{1,0:T(8,128)(2,1)S(1)}, bf16[256,256]{1,0:T(8,128)(2,1)S(1)}, u32[]{:S(2)}, u32[]{:S(2)}) collective-permute-start(bf16[256,256]{1,0:T(8,128)(2,1)S(1)} %get-tuple-element.59), channel_id=1, source_target_pairs={{0,31},{1,2},{2,1},{3,4},{4,3},{5,6},{6,5},{7,8},{8,7},{9,10},{10,... | collective-permute-start | bytes 393224 | tf_op jit(solution)/shard_map/ppermute | solution.py:234
  18.7 0.0 collective-permute-start.5
  18.7 0.8 %shard_map.107 = (f32[512,256]{1,0:T(8,128)S(1)}, f32[512,256]{1,0:T(8,128)S(1)}) custom-call(bf16[128,256]{1,0:T(8,128)(2,1)S(1)} %collective-permute-done.near, bf16[128,256]{1,0:T(8,128)(2,1)S(1)} %collective-permute-done.1.far, bf16[256,256]{1,0:T(8,128)(2,1)S(1)} %collective-permute-done.2.wide, f32[512,256]{1,0:T(8,128)S(1)} %get-tuple-element.61.local, ...), custom_call_target="tpu_custom_call" | custom-call | tf_op jit(solution)/shard_map/pallas_call | solution.py:303
  19.6 4.0 %collective-permute-done.4.far = bf16[256,256]{1,0:T(8,128)(2,1)S(1)} collective-permute-done((bf16[256,256]{1,0:T(8,128)(2,1)S(1)}, bf16[256,256]{1,0:T(8,128)(2,1)S(1)}, u32[]{:S(2)}, u32[]{:S(2)}) %collective-permute-start.4) | collective-permute-done | bytes 131104 | tf_op jit(solution)/shard_map/ppermute | solution.py:234
  23.6 2.8 %collective-permute-done.5.wide = bf16[256,256]{1,0:T(8,128)(2,1)S(1)} collective-permute-done((bf16[256,256]{1,0:T(8,128)(2,1)S(1)}, bf16[256,256]{1,0:T(8,128)(2,1)S(1)}, u32[]{:S(2)}, u32[]{:S(2)}) %collective-permute-start.5) | collective-permute-done | bytes 131104 | tf_op jit(solution)/shard_map/ppermute | solution.py:219
  26.4 0.5 shard_map.108
  26.9 0.8 %collective-permute-start.8 = (bf16[256,256]{1,0:T(8,128)(2,1)S(1)}, bf16[256,256]{1,0:T(8,128)(2,1)S(1)}, u32[]{:S(2)}, u32[]{:S(2)}) collective-permute-start(bf16[256,256]{1,0:T(8,128)(2,1)S(1)} %get-tuple-element.68), channel_id=1, source_target_pairs={{0,16},{1,17},{2,18},{3,19},{4,20},{5,21},{6,22},{7,23},{8,24},{9,... | collective-permute-start | bytes 393224 | tf_op jit(solution)/shard_map/ppermute | solution.py:219
  27.7 0.0 collective-permute-start.6
  27.7 1.9 %collective-permute-start.7 = (bf16[128,256]{1,0:T(8,128)(2,1)S(1)}, bf16[128,256]{1,0:T(8,128)(2,1)S(1)}, u32[]{:S(2)}, u32[]{:S(2)}) collective-permute-start(bf16[128,256]{1,0:T(8,128)(2,1)S(1)} %get-tuple-element.67), channel_id=1, source_target_pairs={{0,31},{1,2},{2,1},{3,4},{4,3},{5,6},{6,5},{7,8},{8,7},{9,10},{10,... | collective-permute-start | bytes 196616 | tf_op jit(solution)/shard_map/ppermute | solution.py:234
  29.6 0.8 %shard_map.109 = (f32[512,256]{1,0:T(8,128)S(1)}, f32[512,256]{1,0:T(8,128)S(1)}) custom-call(bf16[256,256]{1,0:T(8,128)(2,1)S(1)} %collective-permute-done.3.near, bf16[256,256]{1,0:T(8,128)(2,1)S(1)} %collective-permute-done.4.far, bf16[256,256]{1,0:T(8,128)(2,1)S(1)} %collective-permute-done.5.wide, f32[512,256]{1,0:T(8,128)S(1)} %get-tuple-element.69.local, ...), custom_call_target="tpu_custom_call" | custom-call | tf_op jit(solution)/shard_map/pallas_call | solution.py:303
  30.4 0.0 collective-permute-done.6.near
  30.5 4.7 %collective-permute-done.7.far = bf16[128,256]{1,0:T(8,128)(2,1)S(1)} collective-permute-done((bf16[128,256]{1,0:T(8,128)(2,1)S(1)}, bf16[128,256]{1,0:T(8,128)(2,1)S(1)}, u32[]{:S(2)}, u32[]{:S(2)}) %collective-permute-start.7) | collective-permute-done | bytes 65568 | tf_op jit(solution)/shard_map/ppermute | solution.py:234
  35.1 0.5 shard_map.110
  35.6 2.8 %collective-permute-start.11 = (bf16[256,256]{1,0:T(8,128)(2,1)S(1)}, bf16[256,256]{1,0:T(8,128)(2,1)S(1)}, u32[]{:S(2)}, u32[]{:S(2)}) collective-permute-start(bf16[256,256]{1,0:T(8,128)(2,1)S(1)} %get-tuple-element.73), channel_id=1, source_target_pairs={{0,16},{1,17},{2,18},{3,19},{4,20},{5,21},{6,22},{7,23},{8,24},{9,... | collective-permute-start | bytes 393224 | tf_op jit(solution)/shard_map/ppermute | solution.py:219
  38.4 0.2 collective-permute-start.12
  38.6 2.7 %collective-permute-start.13 = (bf16[128,256]{1,0:T(8,128)(2,1)S(1)}, bf16[128,256]{1,0:T(8,128)(2,1)S(1)}, u32[]{:S(2)}, u32[]{:S(2)}) collective-permute-start(bf16[128,256]{1,0:T(8,128)(2,1)S(1)} %get-tuple-element.76), channel_id=1, source_target_pairs={{0,16},{1,17},{2,18},{3,19},{4,20},{5,21},{6,22},{7,23},{8,24},{9,... | collective-permute-start | bytes 196616 | tf_op jit(solution)/shard_map/ppermute | solution.py:228
  41.4 0.0 collective-permute-start.9
  41.4 0.6 collective-permute-start.10
  41.9 5.1 %collective-permute-done.12.wide_a = bf16[128,256]{1,0:T(8,128)(2,1)S(1)} collective-permute-done((bf16[128,256]{1,0:T(8,128)(2,1)S(1)}, bf16[128,256]{1,0:T(8,128)(2,1)S(1)}, u32[]{:S(2)}, u32[]{:S(2)}) %collective-permute-start.12) | collective-permute-done | bytes 65568 | tf_op jit(solution)/shard_map/ppermute | solution.py:228
  47.1 0.7 collective-permute-done.13.wide_b
  47.8 0.4 shard_map.113
  48.2 0.9 %shard_map.111.local = f32[512,256]{1,0:T(8,128)S(1)} custom-call(bf16[128,256]{1,0:T(8,128)(2,1)S(1)} %collective-permute-done.6.near, bf16[128,256]{1,0:T(8,128)(2,1)S(1)} %collective-permute-done.7.far, bf16[256,256]{1,0:T(8,128)(2,1)S(1)} %collective-permute-done.8.wide, f32[512,256]{1,0:T(8,128)S(1)} %get-tuple-element.74.local, ...), custom_call_target="tpu_custom_call" | custom-call | tf_op jit(solution)/shard_map/pallas_call | solution.py:303
  49.1 0.0 collective-permute-done.9.near
  49.1 0.0 collective-permute-done.10.far
  49.1 0.8 %shard_map.114 = (f32[128,256]{1,0:T(8,128)S(1)}, f32[128,256]{1,0:T(8,128)S(1)}) custom-call(bf16[128,256]{1,0:T(8,128)(2,1)S(1)} %collective-permute-done.9.near, bf16[128,256]{1,0:T(8,128)(2,1)S(1)} %collective-permute-done.10.far, bf16[256,256]{1,0:T(8,128)(2,1)S(1)} %collective-permute-done.11.wide, f32[512,256]{1,0:T(8,128)S(1)} %shard_map.111.local, ...), custom_call_target="tpu_custom_call" | custom-call | tf_op jit(solution)/shard_map/pallas_call | solution.py:312
  49.9 0.1 collective-permute-start.14
  50.0 1.3 %collective-permute-done.14 = f32[128,256]{1,0:T(8,128)S(1)} collective-permute-done((f32[128,256]{1,0:T(8,128)S(1)}, f32[128,256]{1,0:T(8,128)S(1)}, u32[]{:S(2)}, u32[]{:S(2)}) %collective-permute-start.14) | collective-permute-done | bytes 131104 | tf_op jit(solution)/shard_map/ppermute | solution.py:243
  51.3 3.2 %collective-permute-start.15 = (bf16[64,256]{1,0:T(8,128)(2,1)S(1)}, bf16[64,256]{1,0:T(8,128)(2,1)S(1)}, u32[]{:S(2)}, u32[]{:S(2)}) collective-permute-start(bf16[64,256]{1,0:T(8,128)(2,1)S(1)} %get-tuple-element.82), channel_id=1, source_target_pairs={{0,17},{1,16},{2,19},{3,18},{4,21},{5,20},{6,23},{7,22},{8,25},{9,... | collective-permute-start | bytes 98312 | tf_op jit(solution)/shard_map/ppermute | solution.py:250
  54.6 0.1 collective-permute-start.16
  54.7 2.4 %collective-permute-done.15 = bf16[64,256]{1,0:T(8,128)(2,1)S(1)} collective-permute-done((bf16[64,256]{1,0:T(8,128)(2,1)S(1)}, bf16[64,256]{1,0:T(8,128)(2,1)S(1)}, u32[]{:S(2)}, u32[]{:S(2)}) %collective-permute-start.15) | collective-permute-done | bytes 32800 | tf_op jit(solution)/shard_map/ppermute | solution.py:250
  57.0 2.6 %collective-permute-done.16 = bf16[64,256]{1,0:T(8,128)(2,1)S(1)} collective-permute-done((bf16[64,256]{1,0:T(8,128)(2,1)S(1)}, bf16[64,256]{1,0:T(8,128)(2,1)S(1)}, u32[]{:S(2)}, u32[]{:S(2)}) %collective-permute-start.16) | collective-permute-done | bytes 32800 | tf_op jit(solution)/shard_map/ppermute | solution.py:250
  59.7 0.1 collective-permute-start.17
  59.8 4.1 %collective-permute-done.17 = bf16[128,256]{1,0:T(8,128)(2,1)S(1)} collective-permute-done((bf16[128,256]{1,0:T(8,128)(2,1)S(1)}, bf16[128,256]{1,0:T(8,128)(2,1)S(1)}, u32[]{:S(2)}, u32[]{:S(2)}) %collective-permute-start.17) | collective-permute-done | bytes 65568 | tf_op jit(solution)/shard_map/ppermute | solution.py:250
  63.9 0.1 collective-permute-start.18
  64.0 4.1 %collective-permute-done.18 = bf16[128,256]{1,0:T(8,128)(2,1)S(1)} collective-permute-done((bf16[128,256]{1,0:T(8,128)(2,1)S(1)}, bf16[128,256]{1,0:T(8,128)(2,1)S(1)}, u32[]{:S(2)}, u32[]{:S(2)}) %collective-permute-start.18) | collective-permute-done | bytes 65568 | tf_op jit(solution)/shard_map/ppermute | solution.py:250
  68.1 0.6 collective-permute-start.19
  68.6 3.6 %collective-permute-done.19 = bf16[128,256]{1,0:T(8,128)(2,1)S(1)} collective-permute-done((bf16[128,256]{1,0:T(8,128)(2,1)S(1)}, bf16[128,256]{1,0:T(8,128)(2,1)S(1)}, u32[]{:S(2)}, u32[]{:S(2)}) %collective-permute-start.19) | collective-permute-done | bytes 65568 | tf_op jit(solution)/shard_map/ppermute | solution.py:250
  72.2 0.2 collective-permute-start.20
  72.4 1.3 %shard_map.112 = f32[512,256]{1,0:T(8,128)} custom-call(bf16[128,256]{1,0:T(8,128)(2,1)S(1)} %collective-permute-done.9.near, bf16[128,256]{1,0:T(8,128)(2,1)S(1)} %collective-permute-done.10.far, bf16[256,256]{1,0:T(8,128)(2,1)S(1)} %collective-permute-done.11.wide, f32[512,256]{1,0:T(8,128)S(1)} %shard_map.111.local, ...), custom_call_target="tpu_custom_call" | custom-call | tf_op jit(solution)/shard_map/pallas_call | solution.py:315
  73.7 0.7 shard_map.115
  (12 shorter events, 0.1 us)
Async XLA Ops:
  2.1 11.4 %collective-permute-start.2 = (bf16[256,256]{1,0:T(8,128)(2,1)S(1)}, bf16[256,256]{1,0:T(8,128)(2,1)S(1)}, u32[]{:S(2)}, u32[]{:S(2)}) collective-permute-start(bf16[256,256]{1,0:T(8,128)(2,1)S(1)} %get-tuple-element.44), channel_id=1, source_target_pairs={{0,16},{1,17},{2,18},{3,19},{4,20},{5,21},{6,22},{7,23},{8,24},{9,... | collective-permute-start | bytes 393224 | tf_op jit(solution)/shard_map/ppermute | solution.py:219
  6.2 6.3 %collective-permute-start = (bf16[128,256]{1,0:T(8,128)(2,1)S(1)}, bf16[128,256]{1,0:T(8,128)(2,1)S(1)}, u32[]{:S(2)}, u32[]{:S(2)}) collective-permute-start(bf16[128,256]{1,0:T(8,128)(2,1)S(1)} %get-tuple-element.42), channel_id=1, source_target_pairs={{0,1},{1,0},{2,3},{3,2},{4,5},{5,4},{6,7},{7,6},{8,9},{9,8},{10,11... | collective-permute-start | bytes 196616 | tf_op jit(solution)/shard_map/ppermute | solution.py:235
  6.2 7.3 %collective-permute-start.1 = (bf16[128,256]{1,0:T(8,128)(2,1)S(1)}, bf16[128,256]{1,0:T(8,128)(2,1)S(1)}, u32[]{:S(2)}, u32[]{:S(2)}) collective-permute-start(bf16[128,256]{1,0:T(8,128)(2,1)S(1)} %get-tuple-element.43), channel_id=1, source_target_pairs={{0,31},{1,2},{2,1},{3,4},{4,3},{5,6},{6,5},{7,8},{8,7},{9,10},{10,... | collective-permute-start | bytes 196616 | tf_op jit(solution)/shard_map/ppermute | solution.py:234
  14.0 5.5 %collective-permute-start.3 = (bf16[256,256]{1,0:T(8,128)(2,1)S(1)}, bf16[256,256]{1,0:T(8,128)(2,1)S(1)}, u32[]{:S(2)}, u32[]{:S(2)}) collective-permute-start(bf16[256,256]{1,0:T(8,128)(2,1)S(1)} %get-tuple-element.58), channel_id=1, source_target_pairs={{0,1},{1,0},{2,3},{3,2},{4,5},{5,4},{6,7},{7,6},{8,9},{9,8},{10,11... | collective-permute-start | bytes 393224 | tf_op jit(solution)/shard_map/ppermute | solution.py:235
  14.1 9.5 %collective-permute-start.4 = (bf16[256,256]{1,0:T(8,128)(2,1)S(1)}, bf16[256,256]{1,0:T(8,128)(2,1)S(1)}, u32[]{:S(2)}, u32[]{:S(2)}) collective-permute-start(bf16[256,256]{1,0:T(8,128)(2,1)S(1)} %get-tuple-element.59), channel_id=1, source_target_pairs={{0,31},{1,2},{2,1},{3,4},{4,3},{5,6},{6,5},{7,8},{8,7},{9,10},{10,... | collective-permute-start | bytes 393224 | tf_op jit(solution)/shard_map/ppermute | solution.py:234
  18.7 7.7 %collective-permute-start.5 = (bf16[256,256]{1,0:T(8,128)(2,1)S(1)}, bf16[256,256]{1,0:T(8,128)(2,1)S(1)}, u32[]{:S(2)}, u32[]{:S(2)}) collective-permute-start(bf16[256,256]{1,0:T(8,128)(2,1)S(1)} %get-tuple-element.60), channel_id=1, source_target_pairs={{0,16},{1,17},{2,18},{3,19},{4,20},{5,21},{6,22},{7,23},{8,24},{9,... | collective-permute-start | bytes 393224 | tf_op jit(solution)/shard_map/ppermute | solution.py:219
  26.9 8.2 %collective-permute-start.8 = (bf16[256,256]{1,0:T(8,128)(2,1)S(1)}, bf16[256,256]{1,0:T(8,128)(2,1)S(1)}, u32[]{:S(2)}, u32[]{:S(2)}) collective-permute-start(bf16[256,256]{1,0:T(8,128)(2,1)S(1)} %get-tuple-element.68), channel_id=1, source_target_pairs={{0,16},{1,17},{2,18},{3,19},{4,20},{5,21},{6,22},{7,23},{8,24},{9,... | collective-permute-start | bytes 393224 | tf_op jit(solution)/shard_map/ppermute | solution.py:219
  27.7 2.7 %collective-permute-start.6 = (bf16[128,256]{1,0:T(8,128)(2,1)S(1)}, bf16[128,256]{1,0:T(8,128)(2,1)S(1)}, u32[]{:S(2)}, u32[]{:S(2)}) collective-permute-start(bf16[128,256]{1,0:T(8,128)(2,1)S(1)} %get-tuple-element.66), channel_id=1, source_target_pairs={{0,1},{1,0},{2,3},{3,2},{4,5},{5,4},{6,7},{7,6},{8,9},{9,8},{10,11... | collective-permute-start | bytes 196616 | tf_op jit(solution)/shard_map/ppermute | solution.py:235
  27.7 7.4 %collective-permute-start.7 = (bf16[128,256]{1,0:T(8,128)(2,1)S(1)}, bf16[128,256]{1,0:T(8,128)(2,1)S(1)}, u32[]{:S(2)}, u32[]{:S(2)}) collective-permute-start(bf16[128,256]{1,0:T(8,128)(2,1)S(1)} %get-tuple-element.67), channel_id=1, source_target_pairs={{0,31},{1,2},{2,1},{3,4},{4,3},{5,6},{6,5},{7,8},{8,7},{9,10},{10,... | collective-permute-start | bytes 196616 | tf_op jit(solution)/shard_map/ppermute | solution.py:234
  35.6 13.5 %collective-permute-start.11 = (bf16[256,256]{1,0:T(8,128)(2,1)S(1)}, bf16[256,256]{1,0:T(8,128)(2,1)S(1)}, u32[]{:S(2)}, u32[]{:S(2)}) collective-permute-start(bf16[256,256]{1,0:T(8,128)(2,1)S(1)} %get-tuple-element.73), channel_id=1, source_target_pairs={{0,16},{1,17},{2,18},{3,19},{4,20},{5,21},{6,22},{7,23},{8,24},{9,... | collective-permute-start | bytes 393224 | tf_op jit(solution)/shard_map/ppermute | solution.py:219
  38.4 8.7 %collective-permute-start.12 = (bf16[128,256]{1,0:T(8,128)(2,1)S(1)}, bf16[128,256]{1,0:T(8,128)(2,1)S(1)}, u32[]{:S(2)}, u32[]{:S(2)}) collective-permute-start(bf16[128,256]{1,0:T(8,128)(2,1)S(1)} %get-tuple-element.75), channel_id=1, source_target_pairs={{0,16},{1,17},{2,18},{3,19},{4,20},{5,21},{6,22},{7,23},{8,24},{9,... | collective-permute-start | bytes 196616 | tf_op jit(solution)/shard_map/ppermute | solution.py:228
  38.6 9.2 %collective-permute-start.13 = (bf16[128,256]{1,0:T(8,128)(2,1)S(1)}, bf16[128,256]{1,0:T(8,128)(2,1)S(1)}, u32[]{:S(2)}, u32[]{:S(2)}) collective-permute-start(bf16[128,256]{1,0:T(8,128)(2,1)S(1)} %get-tuple-element.76), channel_id=1, source_target_pairs={{0,16},{1,17},{2,18},{3,19},{4,20},{5,21},{6,22},{7,23},{8,24},{9,... | collective-permute-start | bytes 196616 | tf_op jit(solution)/shard_map/ppermute | solution.py:228
  41.4 7.7 %collective-permute-start.9 = (bf16[128,256]{1,0:T(8,128)(2,1)S(1)}, bf16[128,256]{1,0:T(8,128)(2,1)S(1)}, u32[]{:S(2)}, u32[]{:S(2)}) collective-permute-start(bf16[128,256]{1,0:T(8,128)(2,1)S(1)} %get-tuple-element.71), channel_id=1, source_target_pairs={{0,1},{1,0},{2,3},{3,2},{4,5},{5,4},{6,7},{7,6},{8,9},{9,8},{10,11... | collective-permute-start | bytes 196616 | tf_op jit(solution)/shard_map/ppermute | solution.py:235
  41.4 7.8 %collective-permute-start.10 = (bf16[128,256]{1,0:T(8,128)(2,1)S(1)}, bf16[128,256]{1,0:T(8,128)(2,1)S(1)}, u32[]{:S(2)}, u32[]{:S(2)}) collective-permute-start(bf16[128,256]{1,0:T(8,128)(2,1)S(1)} %get-tuple-element.72), channel_id=1, source_target_pairs={{0,31},{1,2},{2,1},{3,4},{4,3},{5,6},{6,5},{7,8},{8,7},{9,10},{10,... | collective-permute-start | bytes 196616 | tf_op jit(solution)/shard_map/ppermute | solution.py:234
  49.9 1.4 %collective-permute-start.14 = (f32[128,256]{1,0:T(8,128)S(1)}, f32[128,256]{1,0:T(8,128)S(1)}, u32[]{:S(2)}, u32[]{:S(2)}) collective-permute-start(f32[128,256]{1,0:T(8,128)S(1)} %get-tuple-element.81), channel_id=1, source_target_pairs={{0,1},{1,0},{2,3},{3,2},{4,5},{5,4},{6,7},{7,6},{8,9},{9,8},{10,11... | collective-permute-start | bytes 393224 | tf_op jit(solution)/shard_map/ppermute | solution.py:243
  51.3 5.7 %collective-permute-start.15 = (bf16[64,256]{1,0:T(8,128)(2,1)S(1)}, bf16[64,256]{1,0:T(8,128)(2,1)S(1)}, u32[]{:S(2)}, u32[]{:S(2)}) collective-permute-start(bf16[64,256]{1,0:T(8,128)(2,1)S(1)} %get-tuple-element.82), channel_id=1, source_target_pairs={{0,17},{1,16},{2,19},{3,18},{4,21},{5,20},{6,23},{7,22},{8,25},{9,... | collective-permute-start | bytes 98312 | tf_op jit(solution)/shard_map/ppermute | solution.py:250
  54.6 5.1 %collective-permute-start.16 = (bf16[64,256]{1,0:T(8,128)(2,1)S(1)}, bf16[64,256]{1,0:T(8,128)(2,1)S(1)}, u32[]{:S(2)}, u32[]{:S(2)}) collective-permute-start(bf16[64,256]{1,0:T(8,128)(2,1)S(1)} %get-tuple-element.83), channel_id=1, source_target_pairs={{0,17},{1,16},{2,19},{3,18},{4,21},{5,20},{6,23},{7,22},{8,25},{9,... | collective-permute-start | bytes 98312 | tf_op jit(solution)/shard_map/ppermute | solution.py:250
  59.7 4.2 %collective-permute-start.17 = (bf16[128,256]{1,0:T(8,128)(2,1)S(1)}, bf16[128,256]{1,0:T(8,128)(2,1)S(1)}, u32[]{:S(2)}, u32[]{:S(2)}) collective-permute-start(bf16[128,256]{1,0:T(8,128)(2,1)S(1)} %add_convert_fusion.2), channel_id=1, source_target_pairs={{0,9},{1,8},{2,11},{3,10},{4,13},{5,12},{6,15},{7,14},{8,1},{9,0},... | collective-permute-start | bytes 196616 | tf_op jit(solution)/shard_map/ppermute | solution.py:250
  63.9 4.2 %collective-permute-start.18 = (bf16[128,256]{1,0:T(8,128)(2,1)S(1)}, bf16[128,256]{1,0:T(8,128)(2,1)S(1)}, u32[]{:S(2)}, u32[]{:S(2)}) collective-permute-start(bf16[128,256]{1,0:T(8,128)(2,1)S(1)} %add_convert_fusion.1), channel_id=1, source_target_pairs={{0,5},{1,4},{2,7},{3,6},{4,1},{5,0},{6,3},{7,2},{8,13},{9,12},{10,... | collective-permute-start | bytes 196616 | tf_op jit(solution)/shard_map/ppermute | solution.py:250
  68.1 4.2 %collective-permute-start.19 = (bf16[128,256]{1,0:T(8,128)(2,1)S(1)}, bf16[128,256]{1,0:T(8,128)(2,1)S(1)}, u32[]{:S(2)}, u32[]{:S(2)}) collective-permute-start(bf16[128,256]{1,0:T(8,128)(2,1)S(1)} %add_convert_fusion), channel_id=1, source_target_pairs={{0,3},{1,2},{2,1},{3,0},{4,7},{5,6},{6,5},{7,4},{8,11},{9,10},{10,... | collective-permute-start | bytes 196616 | tf_op jit(solution)/shard_map/ppermute | solution.py:250
  72.2 1.5 %collective-permute-start.20 = (f32[128,256]{1,0:T(8,128)S(1)}, f32[128,256]{1,0:T(8,128)S(1)}, u32[]{:S(2)}, u32[]{:S(2)}) collective-permute-start(f32[128,256]{1,0:T(8,128)S(1)} %convert_add_fusion.total), channel_id=1, source_target_pairs={{0,1},{1,0},{2,3},{3,2},{4,5},{5,4},{6,7},{7,6},{8,9},{9,8},{10,11... | collective-permute-start | bytes 393224 | tf_op jit(solution)/shard_map/ppermute | solution.py:252
